TPU v7x, 256 devices: a whole 4x4x8 slice. The times are simulated.
256 devices in a mesh: seq: 64 (over x, z_hi, y), rep: 4 (over z_lo, core).
Axes of the slice: x: 4, y: 4, z: 8 (z_hi: 4, z_lo: 2; z = z_hi * 2 + z_lo), core: 2. Of those that a mesh axis runs over, the one named last changes fastest.
Arguments:
- tokens: bfloat16 [8192, 2048], P('seq'), may hold values from -6 to 6
- prior_cache: bfloat16 [2048, 576], P('seq'), may hold values from -6 to 6
- attn_gain: float32 [2048], replicated, may hold values from 0.25 to 1.75
- q_weight: bfloat16 [2048, 1536], P(None, 'rep'), may hold values from -0.125 to 0.125
- kv_weight: bfloat16 [2048, 576], replicated, may hold values from -0.125 to 0.125
- kv_gain: float32 [512], replicated, may hold values from 0.25 to 1.75
- key_up: bfloat16 [8, 128, 512], P('rep'), may hold values from -18.561553006146873 to 18.561553006146873
- value_up: bfloat16 [8, 512, 128], P('rep'), may hold values from -0.25 to 0.25
- out_weight: bfloat16 [1024, 2048], P('rep'), may hold values from -0.1875 to 0.1875
- moe_gain: float32 [2048], replicated, may hold values from 0.25 to 1.75
- router: bfloat16 [2048, 64], replicated, may hold values from -0.125 to 0.125
- expert_ids: int32 [8192, 6], P('seq'), may hold values from 0 to 63, all different within a row; in each aligned block of 32 rows (0 to 31, 32 to 63, ...) at most 4 rows name the same one
- w_gate: bfloat16 [64, 2048, 1408], P('seq', None, 'rep'), may hold values from -0.125 to 0.125
- w_up: bfloat16 [64, 2048, 1408], P('seq', None, 'rep'), may hold values from -0.125 to 0.125
- w_down: bfloat16 [64, 1408, 2048], P('seq', 'rep'), may hold values from -0.15625 to 0.15625
- handover: bfloat16 [256, 1, 1024, 576], P('rep', None, 'seq'), may hold values from -6 to 6
- lengths: int32 [256], replicated, may hold values from 1 to 1024, 65536 in all
- request_owner: int32 [256], replicated, may hold values from 0 to 63, as said below
- page_table: int32 [256, 8], replicated, may hold values from 0 to 7, as said below
Outputs:
- layer_out: bfloat16 [8192, 2048], P(('seq', 'rep'))
- decode_pages: bfloat16 [2048, 1, 128, 576], P(('seq', 'rep'))
Inputs may be any that keep to these rules, and one draw needn't show every extreme that they name: `request_owner`: the requests form 4 consecutive groups of 256 / 4; within each group every value is taken by exactly 1 request. `page_table`: for the requests of one group with the same owner, the entries of their rows together are each of 0 to 7 once. `expert_ids`: each row names 6 different experts; in each aligned block of 32 rows no expert is named by more than 4 rows, a bound that some block reaches. The lengths sum to 65536; the largest is 1024.
All inputs are finite; a program needn't handle non-finite values.
Results may differ from a plain program's by a relative error of at most 0.035.
Values may be sent and summed in bfloat16 or wider, within the bound.
A program may use at most 128 MiB of HBM per device.

v0:
```python
import jax
import jax.numpy as jnp
from jax import lax
from jax.sharding import PartitionSpec as P

PAGE = 128


epsilon = 1e-06
rope_base = 50000.0
route_scale = 2.446


def cut_along(value, dim, peers):
    lengths = value.shape
    pieces = value.reshape(*lengths[:dim], peers, lengths[dim] // peers, *lengths[dim + 1 :])
    return jnp.moveaxis(pieces, dim, 0)


def sent_and_summed(value, axis, dim):
    pieces = cut_along(value, dim, lax.axis_size(axis))
    arrived = lax.all_to_all(pieces, axis, split_axis=0, concat_axis=0, tiled=True)
    return arrived.astype(jnp.float32).sum(axis=0)


def rms_scale(values, gain_vector):
    return (
        values
        * lax.rsqrt(jnp.mean(values * values, axis=-1, keepdims=True) + epsilon)
        * gain_vector
    )


def rotate(values, positions):
    half_width = values.shape[-1] // 2
    frequency = rope_base ** (-jnp.arange(half_width).astype(jnp.float32) / half_width)
    angles = (
        positions.astype(jnp.float32).reshape((-1,) + (1,) * (values.ndim - 2) + (1,)) * frequency
    )
    cosine = jnp.cos(angles)
    sine_values = jnp.sin(angles)
    front_half = values[..., :half_width]
    back_half = values[..., half_width:]
    return jnp.concatenate(
        [
            front_half * cosine - back_half * sine_values,
            back_half * cosine + front_half * sine_values,
        ],
        axis=-1,
    )


def latent_keys(row_block, positions, kv_weight, kv_gain, latent_width):
    latent = jnp.dot(row_block, kv_weight, preferred_element_type=jnp.float32)
    return jnp.concatenate(
        [rms_scale(latent[:, :latent_width], kv_gain), rotate(latent[:, latent_width:], positions)],
        axis=1,
    ).astype(jnp.bfloat16)


def slot_table(route_ids, experts_total, capacity):
    blocks_here = route_ids.shape[0]
    flat_ids = route_ids.reshape(blocks_here, -1)
    onehot = (flat_ids[:, :, None] == jnp.arange(experts_total)[None, None, :]).astype(jnp.int32)
    row_ranks = jnp.sum((jnp.cumsum(onehot, axis=1) - 1) * onehot, axis=2)
    return flat_ids * capacity + row_ranks


def source_rows(target, slot_count):
    matches = (target[:, None, :] == jnp.arange(slot_count)[None, :, None]).astype(jnp.int32)
    return (jnp.argmax(matches, axis=2), jnp.max(matches, axis=2))


def on_device(
    tokens,
    prior_cache,
    attn_gain,
    q_weight,
    kv_weight,
    kv_gain,
    key_up,
    value_up,
    out_weight,
    moe_gain,
    router,
    expert_ids,
    w_gate,
    w_up,
    w_down,
    handover,
    lengths,
    request_owner,
    page_table,
):
    seq_count = lax.axis_size("seq")
    rep_count = lax.axis_size("rep")
    seq_index = lax.axis_index("seq")
    rep_index = lax.axis_index("rep")
    tok_dev = tokens.shape[0]
    quarter = tok_dev // rep_count
    prior_dev = prior_cache.shape[0]
    local_heads = key_up.shape[0]
    nope_width = key_up.shape[1]
    latent_width = key_up.shape[2]
    rope_width = q_weight.shape[1] // local_heads - nope_width
    prior_total = prior_dev * seq_count
    token_float = tokens.astype(jnp.float32)
    normed = rms_scale(token_float, attn_gain).astype(jnp.bfloat16)
    span_pos = seq_index * tok_dev + jnp.arange(tok_dev)
    positions = prior_total + span_pos
    projected = jnp.dot(normed, q_weight, preferred_element_type=jnp.float32).reshape(
        tok_dev, local_heads, nope_width + rope_width
    )
    q_nope = projected[..., :nope_width].astype(jnp.bfloat16)
    q_rope = rotate(projected[..., nope_width:], positions)
    q_latent = jnp.einsum("thn,hnc->htc", q_nope, key_up, preferred_element_type=jnp.float32)
    queries = (
        jnp.concatenate([q_latent, jnp.transpose(q_rope, (1, 0, 2))], axis=2)
        .astype(jnp.bfloat16)
        .reshape(local_heads * tok_dev, latent_width + rope_width)
    )
    query_rows_pos = jnp.tile(span_pos, local_heads)
    score_scale = (nope_width + rope_width) ** (-0.5)
    row_count = local_heads * tok_dev
    block_keys = jnp.concatenate(
        [prior_cache, latent_keys(normed, positions, kv_weight, kv_gain, latent_width)], axis=0
    )
    key_piece = lax.all_gather(block_keys, "seq", axis=0, tiled=True)
    running_max = jnp.full((row_count, 1), -1e30, jnp.float32)
    block_rows = prior_dev + tok_dev
    key_index = jnp.arange(key_piece.shape[0])
    owner_block = key_index // block_rows
    within = key_index % block_rows
    key_pos = jnp.where(within < prior_dev, -1, owner_block * tok_dev + within - prior_dev)
    scores = (
        lax.dot_general(
            queries, key_piece, (((1,), (1,)), ((), ())), preferred_element_type=jnp.float32
        )
        * score_scale
    )
    scores = jnp.where(key_pos[None, :] <= query_rows_pos[:, None], scores, -1e30)
    new_max = jnp.maximum(running_max, jnp.max(scores, axis=1, keepdims=True))
    weight = jnp.exp(scores - new_max)
    running_sum = jnp.sum(weight, axis=1, keepdims=True)
    summed = jnp.dot(
        weight.astype(jnp.bfloat16), key_piece[:, :latent_width], preferred_element_type=jnp.float32
    )
    head_latent = (
        (summed / running_sum).astype(jnp.bfloat16).reshape(local_heads, tok_dev, latent_width)
    )
    heads_out = (
        jnp.einsum("htc,hcv->thv", head_latent, value_up, preferred_element_type=jnp.float32)
        .astype(jnp.bfloat16)
        .reshape(tok_dev, -1)
    )
    head_partial = jnp.dot(heads_out, out_weight, preferred_element_type=jnp.float32)
    experts_total = router.shape[1]
    local_experts = w_gate.shape[0]
    top_count = expert_ids.shape[1]
    capacity = max(2, min(quarter, 4 * quarter * top_count // (3 * experts_total)))
    slot_count = experts_total * capacity
    target = slot_table(expert_ids.reshape(rep_count, quarter, top_count), experts_total, capacity)
    own_target = lax.dynamic_index_in_dim(target, rep_index, 0, keepdims=False)
    model_width = tokens.shape[1]
    attention = sent_and_summed(head_partial.astype(jnp.bfloat16), "rep", 0)
    hidden_own = lax.dynamic_slice_in_dim(token_float, rep_index * quarter, quarter, 0) + attention
    moe_own = rms_scale(hidden_own, moe_gain).astype(jnp.bfloat16)
    rows_from, live_mask = source_rows(own_target[None, :], slot_count)
    token_of = (rows_from // top_count).reshape(1, experts_total, capacity).transpose(1, 0, 2)
    live_mask = live_mask.reshape(1, experts_total, capacity).transpose(1, 0, 2)
    outgoing = jnp.where(
        live_mask[..., None] > 0, jnp.take(moe_own, token_of, axis=0), jnp.zeros((), jnp.bfloat16)
    )
    group_size = handover.shape[0]
    req_dev = group_size // seq_count
    owner_here = lax.dynamic_slice_in_dim(request_owner, rep_index * group_size, group_size, 0)
    request_index = jnp.arange(group_size)
    earlier = jnp.sum(
        (
            (owner_here[None, :] == owner_here[:, None])
            & (request_index[None, :] < request_index[:, None])
        ).astype(jnp.int32),
        axis=1,
    )
    order_key = owner_here * req_dev + earlier
    picked = jnp.argmax((order_key[None, :] == request_index[:, None]).astype(jnp.int32), axis=1)
    parcel = jnp.take(handover, picked, axis=0)
    arrived, parcels = (
        lax.all_to_all(outgoing, "seq", split_axis=0, concat_axis=0, tiled=True),
        lax.all_to_all(parcel, "seq", split_axis=0, concat_axis=0, tiled=True),
    )
    expert_rows = arrived.reshape(
        seq_count, local_experts, outgoing.shape[1], capacity, model_width
    )
    expert_rows = lax.all_gather(expert_rows, "rep", axis=2, tiled=True)
    gate_sum = jnp.einsum(
        "slqcd,ldf->slqcf", expert_rows, w_gate, preferred_element_type=jnp.float32
    )
    up_sum = jnp.einsum("slqcd,ldf->slqcf", expert_rows, w_up, preferred_element_type=jnp.float32)
    activated = (jax.nn.silu(gate_sum) * up_sum).astype(jnp.bfloat16)
    expert_out = jnp.einsum(
        "slqcf,lfd->slqcd", activated, w_down, preferred_element_type=jnp.float32
    )
    expert_share = lax.psum_scatter(
        expert_out.astype(jnp.bfloat16), "rep", scatter_dimension=2, tiled=True
    )
    returned = lax.all_to_all(expert_share, "seq", split_axis=0, concat_axis=0, tiled=True).reshape(
        slot_count, model_width
    )
    own_ids = lax.dynamic_slice_in_dim(expert_ids, rep_index * quarter, quarter, 0)
    logits = jnp.dot(moe_own, router, preferred_element_type=jnp.float32)
    chosen = jnp.take_along_axis(logits, own_ids, axis=1)
    gate_score = jax.nn.sigmoid(chosen)
    weights = route_scale * gate_score / jnp.sum(gate_score, axis=1, keepdims=True)
    gathered = jnp.take(returned, own_target, axis=0).reshape(quarter, top_count, model_width)
    moe_sum = jnp.sum(weights[..., None] * gathered.astype(jnp.float32), axis=1)
    layer_out = (hidden_own + moe_sum).astype(jnp.bfloat16)
    layers_here = handover.shape[1]
    pos_dev = handover.shape[2]
    row_width = handover.shape[3]
    maxlen = seq_count * pos_dev
    pages_per = maxlen // PAGE
    stacked = (
        parcels.reshape(seq_count, req_dev, layers_here, pos_dev, row_width)
        .transpose(1, 2, 0, 3, 4)
        .reshape(req_dev, layers_here, maxlen, row_width)
    )
    own_requests = (
        lax.dynamic_slice_in_dim(picked, seq_index * req_dev, req_dev, 0) + rep_index * group_size
    )
    own_lengths = jnp.take(lengths, own_requests)
    alive_mask = jnp.arange(maxlen)[None, :] < own_lengths[:, None]
    stacked = jnp.where(alive_mask[:, None, :, None], stacked, jnp.zeros((), jnp.bfloat16))
    page_rows = (
        stacked.reshape(req_dev, layers_here, pages_per, PAGE, row_width)
        .transpose(0, 2, 1, 3, 4)
        .reshape(req_dev * pages_per, layers_here, PAGE, row_width)
    )
    physical = jnp.take(page_table, own_requests, axis=0).reshape(-1)
    inverse = jnp.argmax(
        (physical[None, :] == jnp.arange(req_dev * pages_per)[:, None]).astype(jnp.int32), axis=1
    )
    decode_pages = jnp.take(page_rows, inverse, axis=0)
    return (layer_out, decode_pages)


def solution(mesh):
    return jax.shard_map(
        on_device,
        mesh=mesh,
        in_specs=(
            P("seq", None),
            P("seq", None),
            P(),
            P(None, "rep"),
            P(),
            P(),
            P("rep", None, None),
            P("rep", None, None),
            P("rep", None),
            P(),
            P(),
            P("seq", None),
            P("seq", None, "rep"),
            P("seq", None, "rep"),
            P("seq", "rep", None),
            P("rep", None, "seq", None),
            P(),
            P(),
            P(),
        ),
        out_specs=(P(("seq", "rep"), None), P(("seq", "rep"), None, None, None)),
        check_vma=False,
    )
```

profile of v0, /device:TPU:32, one launch (start us, length us, event | category | flops | bytes accessed | tf_op | source)
XLA Modules:
  0.0 447.4 jit_solution(16302384563088852875)
XLA Ops:
  7.3 1.4 multiply_reduce_fusion.1
  8.6 0.3 copy-done
  9.0 1.9 fusion.36
  11.7 0.8 copy.104
  12.6 0.8 fusion.37
  13.8 2.4 reduce-window.6
  16.7 0.5 broadcast.537
  17.3 0.6 fusion.58
  17.9 0.7 convert_reduce_fusion.1
  18.6 0.6 fusion.61
  19.7 140.3 %all-gather.4.cloned.1.call-done = bf16[10240,576]{1,0:T(8,128)(2,1)} async-done(((bf16[160,576]{1,0:T(8,128)(2,1)}), bf16[10240,576]{1,0:T(8,128)(2,1)}) %all-gather.4.cloned.1.call-update) | async-done | bytes 11796496 | tf_op jit(solution)/shard_map/all_gather | solution.py:128
  160.0 16.1 %fusion.62 = (f32[256]{0:T(256)S(1)}, f32[256,10240]{1,0:T(8,128)}) fusion(bf16[10240,576]{1,0:T(8,128)(2,1)} %all-gather.4.cloned.1.call-done, bf16[256,64]{1,0:T(8,128)(2,1)S(1)} %bitcast.145, bf16[256,512]{1,0:T(8,128)(2,1)S(1)} %bitcast.143, s32[256]{0:T(256)S(1)} %broadcast_bitcast_fusion, s32[10240]{0:T(1024)S(1)} %fusion.47), kind=kOutput, calls=%fused_computation.137 | convolution fusion | flops 3030974208 | bytes 22620160 | tf_op jit(solution)/shard_map/dot_general | solution.py:136
  176.1 5.7 %fusion.3 = f32[256]{0:T(256)S(1)} fusion(f32[256,10240]{1,0:T(8,128)} %get-tuple-element.57, f32[256]{0:T(256)S(1)} %broadcast_maximum_fusion), kind=kLoop, calls=%fused_computation.10 | loop fusion | flops 5242624 | bytes 10487808 | tf_op jit(solution)/shard_map/reduce_sum | solution.py:144
  181.8 1.3 copy-done.2
  183.1 7.0 %fusion.24 = bf16[256,512]{1,0:T(8,128)(2,1)S(1)} fusion(bf16[10240,576]{1,0:T(8,128)(2,1)} %all-gather.4.cloned.1.call-done, f32[256,10240]{1,0:T(8,128)S(1)} %copy-done.2, f32[256]{0:T(256)S(1)} %broadcast_maximum_fusion, f32[256]{0:T(256)S(1)} %fusion.3), kind=kOutput, calls=%fused_computation.35 | convolution fusion | flops 2689859584 | bytes 21235712 | tf_op jit(solution)/shard_map/dot_general | solution.py:145
  190.4 1.1 convolution_convert_fusion
  191.5 3.5 all-to-all-start
  195.8 6.1 %all-to-all-done = bf16[4,32,2048]{2,1,0:T(8,128)(2,1)S(1)} async-done(((bf16[4,32,2048]{2,1,0:T(8,128)(2,1)}), bf16[4,32,2048]{2,1,0:T(8,128)(2,1)S(1)}, u32[]{:S(2)}, u32[]{:S(2)}) %all-to-all-start) | async-done | bytes 524320 | tf_op jit(solution)/shard_map/all_to_all | solution.py:22
  202.2 0.7 copy-done.4
  203.0 1.4 gather_fusion
  204.4 0.4 reshape.543
  204.8 0.8 select_bitcast_fusion.1
  205.6 39.1 %all_to_all.20 = bf16[64,1,4,2048]{3,2,1,0:T(4,128)(2,1)S(1)} all-to-all(bf16[64,1,4,2048]{3,2,1,0:T(4,128)(2,1)S(1)} %select_bitcast_fusion.1), channel_id=1, replica_groups=mesh['seq'=64,'rep'=4] {'seq'}, dimensions={0} | all-to-all | bytes 2097152 | tf_op jit(solution)/shard_map/all_to_all | solution.py:189
  244.7 1.5 copy.119
  246.3 45.4 %all-gather.6.cloned.1.call-done = bf16[64,4,4,2048]{3,0,2,1:T(8,128)(2,1)} async-done(((bf16[64,1,4,2048]{3,0,2,1:T(8,128)(2,1)}), bf16[64,4,4,2048]{3,0,2,1:T(8,128)(2,1)}) %all-gather.6.cloned.1.call-update) | async-done | bytes 4194320 | tf_op jit(solution)/shard_map/all_gather | solution.py:195
  291.7 6.2 %fusion.13 = f32[64,4,4,352]{3,0,2,1:T(8,128)} fusion(bf16[64,4,4,2048]{3,0,2,1:T(8,128)(2,1)} %all-gather.6.cloned.1.call-done, bf16[1,2048,352]{1,2,0:T(8,128)(2,1)} %param.31), kind=kOutput, calls=%fused_computation.25 | convolution fusion | flops 1476395008 | bytes 7077888 | tf_op jit(solution)/shard_map/slqcd,ldf->slqcf/dot_general | solution.py:196
  297.9 9.5 %convert_bitcast_fusion = bf16[64,1,4,4,2048]{4,0,3,2,1:T(8,128)(2,1)} fusion(bf16[1,352,2048]{2,1,0:T(8,128)(2,1)S(1)} %copy-done.17, bf16[64,4,4,2048]{3,0,2,1:T(8,128)(2,1)} %all-gather.6.cloned.1.call-done, bf16[1,2048,352]{1,2,0:T(8,128)(2,1)} %param.32, f32[64,4,4,352]{3,0,2,1:T(8,128)} %fusion.13), kind=kOutput, calls=%fused_computation.13 | convolution fusion | flops 2957049856 | bytes 12713984 | tf_op jit(solution)/shard_map/slqcf,lfd->slqcd/dot_general | solution.py:201
  307.4 0.6 copy-done.16
  308.4 0.6 iota_reduce_fusion
  309.1 2.1 gather_fusion.2
  311.2 1.3 bitcast_select_fusion
  312.5 13.0 %all-to-all-start.3 = ((bf16[64,1,16,576]{3,2,1,0:T(8,128)(2,1)}), bf16[64,1,16,576]{3,2,1,0:T(8,128)(2,1)S(1)}, u32[]{:S(2)}, u32[]{:S(2)}) async-start(bf16[64,1,16,576]{3,2,1,0:T(8,128)(2,1)} %bitcast_select_fusion), calls=%async_computation.4 | async-start | bytes 2621440 | tf_op jit(solution)/shard_map/all_to_all | solution.py:190
  325.7 0.6 dynamic_slice.20
  326.9 0.6 dynamic-slice.6
  328.3 55.7 %reduce-scatter.2.cloned.1.call-done = bf16[64,1,1,4,2048]{4,0,3,2,1:T(8,128)(2,1)} async-done(((bf16[64,1,4,4,2048]{4,0,3,2,1:T(8,128)(2,1)}), bf16[64,1,1,4,2048]{4,0,3,2,1:T(8,128)(2,1)}) %reduce-scatter.2.cloned.1.call-update) | async-done | bytes 1048592 | tf_op jit(solution)/shard_map/reduce_scatter | solution.py:204
  384.0 3.0 copy.120
  387.0 14.1 %all-to-all-start.2 = ((bf16[64,1,1,4,2048]{4,3,2,1,0:T(4,128)(2,1)}), bf16[64,1,1,4,2048]{4,3,2,1,0:T(4,128)(2,1)}, u32[]{:S(2)}, u32[]{:S(2)}) async-start(bf16[64,1,1,4,2048]{4,3,2,1,0:T(4,128)(2,1)} %copy.120), calls=%async_computation.3 | async-start | bytes 2097152 | tf_op jit(solution)/shard_map/all_to_all | solution.py:207
  401.6 0.6 iota_reduce_fusion.1
  402.3 0.8 copy.121
  403.2 0.8 gather_fusion.3
  404.0 1.2 fusion.18
  405.4 1.6 gather_fusion.4
  407.4 25.3 %all-to-all-done.2 = bf16[64,1,1,4,2048]{4,3,2,1,0:T(4,128)(2,1)} async-done(((bf16[64,1,1,4,2048]{4,3,2,1,0:T(4,128)(2,1)}), bf16[64,1,1,4,2048]{4,3,2,1,0:T(4,128)(2,1)}, u32[]{:S(2)}, u32[]{:S(2)}) %all-to-all-start.2) | async-done | bytes 1048608 | tf_op jit(solution)/shard_map/all_to_all | solution.py:207
  432.7 1.3 reshape.493
  434.1 2.0 gather_fusion.1
  436.1 1.3 gather.33
  437.4 1.7 multiply_reduce_fusion
  439.2 1.6 add_convert_fusion
  (111 shorter events, 5.4 us)
Async XLA Ops:
  7.2 1.8 copy-start
  7.2 152.9 %all-gather.4.cloned.1.call-start = ((), (), s32[]{:S(2)}) async-start(), calls=%async_computation.5 | async-start | bytes 13312000 | tf_op jit(solution)/shard_map/all_gather | solution.py:128
  9.0 2.0 copy-start.10
  9.0 2.4 copy-start.14
  10.9 1.6 copy-start.3
  10.9 1.6 copy-start.5
  10.9 1.6 copy-start.12
  11.7 1.9 copy-start.11
  13.3 6.1 %copy-start.7 = (bf16[2,128,512]{2,1,0:T(8,128)(2,1)S(1)}, bf16[2,128,512]{2,1,0:T(8,128)(2,1)}, u32[]{:S(2)}) copy-start(bf16[2,128,512]{2,1,0:T(8,128)(2,1)} %param.25) | copy-start | bytes 786436
  176.1 7.0 %copy-start.2 = (f32[256,10240]{1,0:T(8,128)S(1)}, f32[256,10240]{1,0:T(8,128)}, u32[]{:S(2)}) copy-start(f32[256,10240]{1,0:T(8,128)} %get-tuple-element.57) | copy-start | bytes 31457284
  183.1 7.0 %copy-start.8 = (bf16[2,512,128]{2,1,0:T(8,128)(2,1)S(1)}, bf16[2,512,128]{2,1,0:T(8,128)(2,1)}, u32[]{:S(2)}) copy-start(bf16[2,512,128]{2,1,0:T(8,128)(2,1)} %param.26) | copy-start | bytes 786436
  183.1 7.3 %copy-start.6 = (bf16[256,2048]{1,0:T(8,128)(2,1)S(1)}, bf16[256,2048]{1,0:T(8,128)(2,1)}, u32[]{:S(2)}) copy-start(bf16[256,2048]{1,0:T(8,128)(2,1)} %param.27) | copy-start | bytes 3145732
  191.5 10.5 %all-to-all-start = ((bf16[4,32,2048]{2,1,0:T(8,128)(2,1)}), bf16[4,32,2048]{2,1,0:T(8,128)(2,1)S(1)}, u32[]{:S(2)}, u32[]{:S(2)}) async-start(bf16[4,32,2048]{2,1,0:T(8,128)(2,1)} %bitcast.8), calls=%async_computation | async-start | bytes 1048576 | tf_op jit(solution)/shard_map/all_to_all | solution.py:22
  195.0 96.7 %all-gather.6.cloned.1.call-start = ((), (), s32[]{:S(2)}) async-start(), calls=%async_computation.7 | async-start | bytes 5242880 | tf_op jit(solution)/shard_map/all_gather | solution.py:195
  195.2 7.7 %copy-start.13 = (f32[2048]{0:T(1024)S(1)}, f32[2048]{0:T(1024)}, u32[]{:S(2)}) copy-start(f32[2048]{0:T(1024)} %param.28) | copy-start | bytes 24580
  202.2 0.7 copy-start.4
  246.2 51.6 %copy-start.17 = (bf16[1,352,2048]{2,1,0:T(8,128)(2,1)S(1)}, bf16[1,352,2048]{2,1,0:T(8,128)(2,1)}, u32[]{:S(2)}) copy-start(bf16[1,352,2048]{2,1,0:T(8,128)(2,1)} %param.33) | copy-start | bytes 4325380
  246.3 137.7 %reduce-scatter.2.cloned.1.call-start = ((), (), s32[]{:S(2)}) async-start(), calls=%async_computation.6 | async-start | bytes 5242880 | tf_op jit(solution)/shard_map/reduce_scatter | solution.py:204
  307.4 0.7 copy-start.16
  312.5 14.5 %copy-start.18 = (s32[256]{0:T(256)S(1)}, s32[256]{0:T(256)}, u32[]{:S(2)}) copy-start(s32[256]{0:T(256)} %param.35) | copy-start | bytes 3076
  312.5 74.6 %all-to-all-start.3 = ((bf16[64,1,16,576]{3,2,1,0:T(8,128)(2,1)}), bf16[64,1,16,576]{3,2,1,0:T(8,128)(2,1)S(1)}, u32[]{:S(2)}, u32[]{:S(2)}) async-start(bf16[64,1,16,576]{3,2,1,0:T(8,128)(2,1)} %bitcast_select_fusion), calls=%async_computation.4 | async-start | bytes 2621440 | tf_op jit(solution)/shard_map/all_to_all | solution.py:190
  387.0 14.4 %copy-start.15 = (s32[256,8]{0,1:T(8,128)S(1)}, s32[256,8]{0,1:T(8,128)}, u32[]{:S(2)}) copy-start(s32[256,8]{0,1:T(8,128)} %param.37) | copy-start | bytes 24580
  387.0 45.7 %all-to-all-start.2 = ((bf16[64,1,1,4,2048]{4,3,2,1,0:T(4,128)(2,1)}), bf16[64,1,1,4,2048]{4,3,2,1,0:T(4,128)(2,1)}, u32[]{:S(2)}, u32[]{:S(2)}) async-start(bf16[64,1,1,4,2048]{4,3,2,1,0:T(4,128)(2,1)} %copy.120), calls=%async_computation.3 | async-start | bytes 2097152 | tf_op jit(solution)/shard_map/all_to_all | solution.py:207
  404.0 1.2 copy-start.9
  434.1 6.8 %copy-start.1 = (bf16[2048,576]{0,1:T(8,128)(2,1)S(1)}, bf16[2048,576]{0,1:T(8,128)(2,1)}, u32[]{:S(2)}) copy-start(bf16[2048,576]{0,1:T(8,128)(2,1)} %param.23) | copy-start | bytes 7077892
Sparse Core Ops, SparseCore 0:
  12.6 147.3 all-gather.3
  246.4 45.2 all-gather.5
  307.6 76.3 reduce-scatter.1
where the time goes:
time: 448 us; the launch traced here: 447 us
  waiting for transfers between devices  273 us (61%)
  matrix products  43.3 us (10%)
  blocking collectives  39.1 us (9%)
  starting transfers between devices  30.9 us (7%)
  local copies, waits for them, and re-layouts  24 us (5%)
  other arithmetic  21.5 us (5%)
  between operations  15.6 us (3%)
    all_gather x1, waiting for transfers between devices, on_device(): key_piece = lax.all_gather(block_keys, 'seq', axis=0, tiled=True)  140 us
    reduce_scatter x1, waiting for transfers between devices, on_device(): lax.psum_scatter(expert_out.astype(jnp.bfloat16), 'rep', scatter_dimensio...  55.7 us
    all_gather x1, waiting for transfers between devices, on_device(): expert_rows = lax.all_gather(expert_rows, 'rep', axis=2, tiled=True)  45.4 us
    all_to_all x1, blocking collectives, on_device(): lax.all_to_all(outgoing, 'seq', split_axis=0, concat_axis=0, tiled=True)  39.1 us
    all_to_all x1, waiting for transfers between devices, on_device(): lax.all_to_all(expert_share, 'seq', split_axis=0, concat_axis=0, tiled=True)  25.3 us
    dot_general x1, matrix products, on_device(): lax.dot_general(queries, key_piece, (((1,), (1,)), ((), ())), preferred_e...  16.1 us
    all_to_all x1, starting transfers between devices, on_device(): lax.all_to_all(expert_share, 'seq', split_axis=0, concat_axis=0, tiled=True)  14.1 us
    all_to_all x1, starting transfers between devices, on_device(): lax.all_to_all(parcel, 'seq', split_axis=0, concat_axis=0, tiled=True)  13 us
  transfers between devices with their start and end apart: 6, of which 5 were waited for; matrix products, arithmetic and copies ran while one was open for 5% of the time, Pallas kernels for 0%

commit v1 on v0

--- a/solution.py
+++ b/solution.py
@@ -1,6 +1,9 @@
+import functools
 import jax
 import jax.numpy as jnp
 from jax import lax
+from jax.experimental import pallas as pl
+from jax.experimental.pallas import tpu as pltpu
 from jax.sharding import PartitionSpec as P
 
 PAGE = 128
@@ -69,6 +72,368 @@
 def source_rows(target, slot_count):
     matches = (target[:, None, :] == jnp.arange(slot_count)[None, :, None]).astype(jnp.int32)
     return (jnp.argmax(matches, axis=2), jnp.max(matches, axis=2))
+
+
+MESH = pl.DeviceIdType.MESH
+HALF = 80
+LATW = 512
+KEYW = 640
+
+
+def remote(src, dst, send_sem, recv_sem, seq, rep):
+    return pltpu.make_async_remote_copy(
+        src_ref=src,
+        dst_ref=dst,
+        send_sem=send_sem,
+        recv_sem=recv_sem,
+        device_id=(seq, rep),
+        device_id_type=MESH,
+    )
+
+
+def greet(partners):
+    barrier = pltpu.get_barrier_semaphore()
+    for seq, rep in partners:
+        pl.semaphore_signal(barrier, inc=1, device_id=(seq, rep), device_id_type=MESH)
+    pl.semaphore_wait(barrier, len(partners))
+
+
+def ring_offset(j):
+    return j + jnp.where(j >= 2, 1, 0) - jnp.where(j >= 3, 2, 0)
+
+
+def attend_kernel(
+    scale,
+    prior_rows,
+    span_rows,
+    q_ref,
+    own_ref,
+    out_ref,
+    ring,
+    sib,
+    acc,
+    mx,
+    sm,
+    local_sem,
+    z_send,
+    z_recv,
+    a_send,
+    a_recv,
+    a2_send,
+    a2_recv,
+    b_send,
+    b_recv,
+    b2_send,
+    b2_recv,
+    s_send,
+    s_recv,
+):
+    seq = lax.axis_index("seq")
+    rep = lax.axis_index("rep")
+    core = lax.rem(rep, 2)
+    zl = rep // 2
+    x0 = seq // 16
+    g = lax.rem(seq // 4, 4)
+    y0 = lax.rem(seq, 4)
+    a0 = x0 + core * (y0 - x0)
+    b0 = y0 + core * (x0 - y0)
+    sa = 16 - 15 * core
+    sb = 1 + 15 * core
+    d = 2 * zl - 1
+    mate = rep + 1 - 2 * core
+    other = rep + 2 - 4 * zl
+
+    def m4(v):
+        return lax.rem(v + 4, 4)
+
+    def seq_of(a, z, b):
+        return a * sa + z * 4 + b * sb
+
+    a_next = seq_of(m4(a0 + 1), g, b0)
+    a_prev = seq_of(m4(a0 - 1), g, b0)
+    b_next = seq_of(a0, g, m4(b0 + 1))
+    b_prev = seq_of(a0, g, m4(b0 - 1))
+    z_to = [
+        (seq_of(a0, m4(g + d), b0), other),
+        (seq_of(a0, m4(g + d), b0), rep),
+        (seq_of(a0, m4(g + 2), b0), other),
+    ]
+    z_in = [m4(g + d), m4(g - d), m4(g + 2)]
+    partners = [
+        (a_next, rep),
+        (a_prev, rep),
+        (b_next, rep),
+        (b_prev, rep),
+        (seq, mate),
+        z_to[0],
+        z_to[1],
+        (seq_of(a0, m4(g - d), b0), rep),
+        z_to[2],
+    ]
+    zs = [g] + z_in
+
+    def place(j):
+        return ring_offset(j)
+
+    own_slot = ring.at[b0, a0, g]
+    local = pltpu.make_async_copy(
+        own_ref.at[pl.ds(pl.multiple_of(core * HALF, HALF), HALF)], own_slot, local_sem.at[0]
+    )
+    local_sib = pltpu.make_async_copy(
+        own_ref.at[pl.ds(pl.multiple_of((1 - core) * HALF, HALF), HALF)],
+        sib.at[a0, b0, g],
+        local_sem.at[1],
+    )
+    local.start()
+    local_sib.start()
+    mx[...] = jnp.full(mx.shape, -1e30, jnp.float32)
+    sm[...] = jnp.zeros(sm.shape, jnp.float32)
+    acc[...] = jnp.zeros(acc.shape, jnp.float32)
+    local.wait()
+    local_sib.wait()
+    greet(partners)
+
+    def z_copy(k):
+        return remote(own_slot, own_slot, z_send.at[k], z_recv.at[k], z_to[k][0], z_to[k][1])
+
+    def z_arrival(k):
+        slot = ring.at[b0, a0, z_in[k]]
+        return remote(slot, slot, z_send.at[k], z_recv.at[k], z_to[k][0], z_to[k][1])
+
+    def a_copy(i, k):
+        slot = ring.at[b0, a0, zs[k]]
+        return remote(slot, slot, a_send.at[i, k], a_recv.at[i, k], (a_next, a_prev)[i], rep)
+
+    def a_arrival(i, k):
+        slot = ring.at[b0, m4(a0 + (-1, 1)[i]), zs[k]]
+        return remote(slot, slot, a_send.at[i, k], a_recv.at[i, k], (a_next, a_prev)[i], rep)
+
+    def a2_copy(k):
+        i = k % 2
+        slot = ring.at[b0, m4(a0 + (-1, 1)[i]), zs[k]]
+        return remote(slot, slot, a2_send.at[k], a2_recv.at[k], (a_next, a_prev)[i], rep)
+
+    def a2_arrival(k):
+        slot = ring.at[b0, m4(a0 + 2), zs[k]]
+        return remote(slot, slot, a2_send.at[k], a2_recv.at[k], (a_next, a_prev)[k % 2], rep)
+
+    def b_copy(i, j, k):
+        slot = ring.at[b0, m4(a0 + place(j)), zs[k]]
+        n = j * 4 + k
+        return remote(slot, slot, b_send.at[i, n], b_recv.at[i, n], (b_next, b_prev)[i], rep)
+
+    def b_arrival(i, j, k):
+        slot = ring.at[m4(b0 + (-1, 1)[i]), m4(a0 + place(j)), zs[k]]
+        n = j * 4 + k
+        return remote(slot, slot, b_send.at[i, n], b_recv.at[i, n], (b_next, b_prev)[i], rep)
+
+    def b2_copy(j, k):
+        i = k % 2
+        slot = ring.at[m4(b0 + (-1, 1)[i]), m4(a0 + place(j)), zs[k]]
+        n = j * 4 + k
+        return remote(slot, slot, b2_send.at[n], b2_recv.at[n], (b_next, b_prev)[i], rep)
+
+    def b2_arrival(j, k):
+        slot = ring.at[m4(b0 + 2), m4(a0 + place(j)), zs[k]]
+        n = j * 4 + k
+        return remote(slot, slot, b2_send.at[n], b2_recv.at[n], (b_next, b_prev)[k % 2], rep)
+
+    def s_copy(h, j, k):
+        bb, aa = m4(b0 + place(h)), m4(a0 + place(j))
+        n = h * 16 + j * 4 + k
+        return remote(
+            ring.at[bb, aa, zs[k]], sib.at[bb, aa, zs[k]], s_send.at[n], s_recv.at[n], seq, mate
+        )
+
+    def s_arrival(h, j, k):
+        bb, aa = m4(a0 + place(h)), m4(b0 + place(j))
+        n = h * 16 + j * 4 + k
+        return remote(
+            ring.at[bb, aa, zs[k]], sib.at[bb, aa, zs[k]], s_send.at[n], s_recv.at[n], seq, mate
+        )
+
+    lane = lax.broadcasted_iota(jnp.int32, (1, 4 * HALF), 1)
+    zblock = (
+        jnp.where(lane >= HALF, 1, 0)
+        + jnp.where(lane >= 2 * HALF, 1, 0)
+        + jnp.where(lane >= 3 * HALF, 1, 0)
+    )
+    within = lane - HALF * zblock
+    qrow = lax.broadcasted_iota(jnp.int32, (q_ref.shape[0], 1), 0)
+    qpos = qrow - jnp.where(qrow >= span_rows, span_rows, 0) + seq * span_rows
+
+    def attend(buf, b, a, stride_a, stride_b, half):
+        keys = buf[b, a].reshape(4 * HALF, KEYW)
+        row = within + half * HALF
+        owner = a * stride_a + b * stride_b + zblock * 4
+        kpos = jnp.where(row < prior_rows, -1, owner * span_rows + row - prior_rows)
+        s = lax.dot_general(
+            q_ref[...], keys, (((1,), (1,)), ((), ())), preferred_element_type=jnp.float32
+        )
+        s = jnp.where(kpos <= qpos, s * scale, -1e30)
+        m_old = mx[:, :1]
+        m_new = jnp.maximum(m_old, jnp.max(s, axis=1, keepdims=True))
+        alpha = jnp.exp(m_old - m_new)
+        p = jnp.exp(s - m_new)
+        sm[...] = sm[...] * alpha + jnp.sum(p, axis=1, keepdims=True)
+        mx[...] = jnp.broadcast_to(m_new, mx.shape)
+        acc[...] = acc[...] * alpha + jnp.dot(
+            p.astype(jnp.bfloat16), keys[:, :LATW], preferred_element_type=jnp.float32
+        )
+
+    def attend_ring(h, j):
+        attend(ring, m4(b0 + place(h)), m4(a0 + place(j)), sa, sb, core)
+
+    def attend_sib(h, j):
+        attend(sib, m4(a0 + place(h)), m4(b0 + place(j)), sb, sa, 1 - core)
+
+    for k in range(3):
+        z_copy(k).start()
+    for i in range(2):
+        a_copy(i, 0).start()
+        b_copy(i, 0, 0).start()
+    for k in (1, 2, 3):
+        z_arrival(k - 1).wait_recv()
+        for i in range(2):
+            a_copy(i, k).start()
+        for i in range(2):
+            b_copy(i, 0, k).start()
+        s_copy(0, 0, k).start()
+    for k in range(4):
+        for i in range(2):
+            a_arrival(i, k).wait_recv()
+            if k % 2 == i:
+                a2_copy(k).start()
+            j = (2, 1)[i]
+            b_copy(0, j, k).start()
+            b_copy(1, j, k).start()
+            s_copy(0, j, k).start()
+    attend_ring(0, 0)
+    for k in range(4):
+        a2_arrival(k).wait_recv()
+        b_copy(0, 3, k).start()
+        b_copy(1, 3, k).start()
+        s_copy(0, 3, k).start()
+    for k in (1, 2, 3):
+        s_arrival(0, 0, k).wait_recv()
+    attend_sib(0, 0)
+
+    def first_b(j, carry):
+        for k in range(4):
+            for i in range(2):
+                b_arrival(i, j, k).wait_recv()
+                if k % 2 == i:
+                    b2_copy(j, k).start()
+                s_copy((2, 1)[i], j, k).start()
+        attend_ring(1, j)
+        attend_ring(2, j)
+        return carry
+
+    def column(j, carry):
+        for k in range(4):
+            s_arrival(0, j, k).wait_recv()
+        attend_ring(0, j)
+        attend_sib(0, j)
+        return carry
+
+    def first_b_sib(j, carry):
+        for h in (1, 2):
+            for k in range(4):
+                s_arrival(h, j, k).wait_recv()
+            attend_sib(h, j)
+        return carry
+
+    def last_b(j, carry):
+        for k in range(4):
+            b2_arrival(j, k).wait_recv()
+            s_copy(3, j, k).start()
+        attend_ring(3, j)
+        return carry
+
+    def last_sib(j, carry):
+        for k in range(4):
+            s_arrival(3, j, k).wait_recv()
+        attend_sib(3, j)
+        return carry
+
+    def middle(j, carry):
+        column(j, carry)
+        first_b(j, carry)
+        return carry
+
+    first_b(0, 0)
+    lax.fori_loop(1, 4, middle, 0)
+
+    def closing(j, carry):
+        first_b_sib(j, carry)
+        last_b(j, carry)
+        return carry
+
+    lax.fori_loop(0, 4, closing, 0)
+    lax.fori_loop(0, 4, last_sib, 0)
+    out_ref[...] = (acc[...] / sm[:, :1]).astype(out_ref.dtype)
+
+    for k in range(3):
+        z_copy(k).wait_send()
+    for k in range(4):
+        for i in range(2):
+            a_copy(i, k).wait_send()
+        a2_copy(k).wait_send()
+
+    def drain(j, carry):
+        for k in range(4):
+            for i in range(2):
+                b_copy(i, j, k).wait_send()
+            b2_copy(j, k).wait_send()
+            for h in (1, 2, 3):
+                s_copy(h, j, k).wait_send()
+        return carry
+
+    lax.fori_loop(0, 4, drain, 0)
+    for k in (1, 2, 3):
+        s_copy(0, 0, k).wait_send()
+
+    def drain_column(j, carry):
+        for k in range(4):
+            s_copy(0, j, k).wait_send()
+        return carry
+
+    lax.fori_loop(1, 4, drain_column, 0)
+
+
+def gathered_attention(queries, own_keys, scale, prior_rows, span_rows):
+    rows = queries.shape[0]
+    dma = pltpu.SemaphoreType.DMA
+    return pl.pallas_call(
+        functools.partial(attend_kernel, scale, prior_rows, span_rows),
+        out_shape=jax.ShapeDtypeStruct((rows, LATW), jnp.bfloat16),
+        in_specs=[pl.BlockSpec(memory_space=pltpu.VMEM)] * 2,
+        out_specs=pl.BlockSpec(memory_space=pltpu.VMEM),
+        scratch_shapes=[
+            pltpu.VMEM((4, 4, 4, HALF, KEYW), jnp.bfloat16),
+            pltpu.VMEM((4, 4, 4, HALF, KEYW), jnp.bfloat16),
+            pltpu.VMEM((rows, LATW), jnp.float32),
+            pltpu.VMEM((rows, 128), jnp.float32),
+            pltpu.VMEM((rows, 128), jnp.float32),
+            dma((2,)),
+            dma((3,)),
+            dma((3,)),
+            dma((2, 4)),
+            dma((2, 4)),
+            dma((4,)),
+            dma((4,)),
+            dma((2, 16)),
+            dma((2, 16)),
+            dma((16,)),
+            dma((16,)),
+            dma((64,)),
+            dma((64,)),
+        ],
+        name="gather_attend",
+        compiler_params=pltpu.CompilerParams(
+            collective_id=0, has_side_effects=True, vmem_limit_bytes=40 << 20
+        ),
+    )(queries, own_keys)
 
 
 def on_device(
@@ -119,35 +484,18 @@
         .astype(jnp.bfloat16)
         .reshape(local_heads * tok_dev, latent_width + rope_width)
     )
-    query_rows_pos = jnp.tile(span_pos, local_heads)
     score_scale = (nope_width + rope_width) ** (-0.5)
-    row_count = local_heads * tok_dev
     block_keys = jnp.concatenate(
         [prior_cache, latent_keys(normed, positions, kv_weight, kv_gain, latent_width)], axis=0
     )
-    key_piece = lax.all_gather(block_keys, "seq", axis=0, tiled=True)
-    running_max = jnp.full((row_count, 1), -1e30, jnp.float32)
-    block_rows = prior_dev + tok_dev
-    key_index = jnp.arange(key_piece.shape[0])
-    owner_block = key_index // block_rows
-    within = key_index % block_rows
-    key_pos = jnp.where(within < prior_dev, -1, owner_block * tok_dev + within - prior_dev)
-    scores = (
-        lax.dot_general(
-            queries, key_piece, (((1,), (1,)), ((), ())), preferred_element_type=jnp.float32
-        )
-        * score_scale
-    )
-    scores = jnp.where(key_pos[None, :] <= query_rows_pos[:, None], scores, -1e30)
-    new_max = jnp.maximum(running_max, jnp.max(scores, axis=1, keepdims=True))
-    weight = jnp.exp(scores - new_max)
-    running_sum = jnp.sum(weight, axis=1, keepdims=True)
-    summed = jnp.dot(
-        weight.astype(jnp.bfloat16), key_piece[:, :latent_width], preferred_element_type=jnp.float32
-    )
-    head_latent = (
-        (summed / running_sum).astype(jnp.bfloat16).reshape(local_heads, tok_dev, latent_width)
-    )
+    spare = KEYW - latent_width - rope_width
+    head_latent = gathered_attention(
+        jnp.pad(queries, ((0, 0), (0, spare))),
+        jnp.pad(block_keys, ((0, 0), (0, spare))),
+        score_scale,
+        prior_dev,
+        tok_dev,
+    ).reshape(local_heads, tok_dev, latent_width)
     heads_out = (
         jnp.einsum("htc,hcv->thv", head_latent, value_up, preferred_element_type=jnp.float32)
         .astype(jnp.bfloat16)

time: 448 us -> 337 us (0.75)
  waiting for transfers between devices: 273 us -> 112 us
  Pallas kernels: 0 us -> 58.3 us
  matrix products: 43.3 us -> 23.3 us
  other arithmetic: 21.5 us -> 26.5 us
    all_gather x1 -> x0, waiting for transfers between devices: 140 us -> none  [on_device(): key_piece = lax.all_gather(block_keys, 'seq', axis=0, tiled=True)]
    pallas_call x0 -> x1, Pallas kernels: none -> 58.3 us  [gathered_attention(): pl.pallas_call(functools.partial(attend_kernel, scale, prior_rows, span_r...]
    dot_general x2 -> x0, matrix products: 23.1 us -> none  [the longest x1 16.1 us: on_device(): lax.dot_general(queries, key_piece, (((1,), (1,)), ((), ())), preferred_e...]
    all_to_all x1, waiting for transfers between devices: 25.3 us -> 17.9 us  [on_device(): lax.all_to_all(expert_share, 'seq', split_axis=0, concat_axis=0, tiled=True)]
    all_to_all x1, waiting for transfers between devices: 6.14 us -> 0.01 us  [sent_and_summed(): lax.all_to_all(pieces, axis, split_axis=0, concat_axis=0, tiled=True)]
    reduce_sum x1 -> x0, other arithmetic: 5.66 us -> none  [on_device(): running_sum = jnp.sum(weight, axis=1, keepdims=True)]
  transfers between devices with their start and end apart: 6 -> 5, of which waited for: 5 -> 3; matrix products, arithmetic and copies ran while one was open for 5% -> 10% of each run, Pallas kernels for 0% -> 0%
where the time goes in v1:
time: 337 us; the launch traced here: 336 us
  waiting for transfers between devices  112 us (33%)
  Pallas kernels  58.3 us (17%)
  blocking collectives  40.5 us (12%)
  starting transfers between devices  31.8 us (9%)
  local copies, waits for them, and re-layouts  28.4 us (8%)
  other arithmetic  26.5 us (8%)
  matrix products  23.3 us (7%)
  between operations  15.8 us (5%)
    pallas_call x1, Pallas kernels, gathered_attention(): pl.pallas_call(functools.partial(attend_kernel, scale, prior_rows, span_r...  58.3 us
    reduce_scatter x1, waiting for transfers between devices, on_device(): lax.psum_scatter(expert_out.astype(jnp.bfloat16), 'rep', scatter_dimensio...  52.3 us
    all_gather x1, waiting for transfers between devices, on_device(): expert_rows = lax.all_gather(expert_rows, 'rep', axis=2, tiled=True)  41.8 us
    all_to_all x1, blocking collectives, on_device(): lax.all_to_all(outgoing, 'seq', split_axis=0, concat_axis=0, tiled=True)  40.5 us
    all_to_all x1, waiting for transfers between devices, on_device(): lax.all_to_all(expert_share, 'seq', split_axis=0, concat_axis=0, tiled=True)  17.9 us
    all_to_all x1, starting transfers between devices, on_device(): lax.all_to_all(expert_share, 'seq', split_axis=0, concat_axis=0, tiled=True)  13.9 us
    all_to_all x1, starting transfers between devices, on_device(): lax.all_to_all(parcel, 'seq', split_axis=0, concat_axis=0, tiled=True)  13.5 us
    dot_general x1, matrix products, on_device(): jnp.einsum('slqcf,lfd->slqcd', activated, w_down, preferred_element_type=...  9.93 us
  transfers between devices with their start and end apart: 5, of which 3 were waited for; matrix products, arithmetic and copies ran while one was open for 10% of the time, Pallas kernels for 0%

profile of v1, /device:TPU:32, one launch (start us, length us, event | category | flops | bytes accessed | tf_op | source)
XLA Modules:
  0.0 336.5 jit_solution(12985275281926456784)
XLA Ops:
  7.2 1.4 multiply_reduce_fusion.1
  9.0 2.1 fusion.26
  11.7 2.2 fusion.27
  13.9 0.6 maximum_bitcast_fusion
  14.5 0.9 copy.116
  15.4 1.3 convolution_convert_fusion.1
  16.9 58.3 %gather_attend.1 = bf16[256,512]{1,0:T(8,128)(2,1)S(1)} custom-call(bf16[256,640]{1,0:T(8,128)(2,1)S(1)} %fusion.20.q_ref, bf16[160,640]{1,0:T(8,128)(2,1)S(1)} %fusion.23.own_ref), custom_call_target="tpu_custom_call" | custom-call | tf_op jit(solution)/shard_map/gather_attend/pallas_call | solution.py:407
  75.5 1.1 convolution_convert_fusion
  76.7 4.4 %all-to-all-start = ((bf16[4,32,2048]{2,1,0:T(8,128)(2,1)}), bf16[4,32,2048]{2,1,0:T(8,128)(2,1)}, u32[]{:S(2)}, u32[]{:S(2)}) async-start(bf16[4,32,2048]{2,1,0:T(8,128)(2,1)} %bitcast.7), calls=%async_computation | async-start | bytes 1048576 | tf_op jit(solution)/shard_map/all_to_all | solution.py:25
  81.4 2.4 reduce-window.6
  84.8 1.2 fusion.35
  86.0 0.7 convert_reduce_fusion.1
  86.7 0.7 fusion.38
  87.5 1.1 convert_element_type.96
  88.9 0.7 gt.26
  89.6 1.1 convert_reduce_fusion
  90.8 1.1 multiply_reduce_fusion.2
  91.9 0.7 copy-done.2
  92.7 1.4 gather_fusion
  94.1 1.2 reshape.511
  95.3 1.9 select_bitcast_fusion.1
  97.2 40.5 %all_to_all.20 = bf16[64,1,4,2048]{3,2,1,0:T(4,128)(2,1)S(1)} all-to-all(bf16[64,1,4,2048]{3,2,1,0:T(4,128)(2,1)S(1)} %select_bitcast_fusion.1), channel_id=1, replica_groups=mesh['seq'=64,'rep'=4] {'seq'}, dimensions={0} | all-to-all | bytes 2097152 | tf_op jit(solution)/shard_map/all_to_all | solution.py:537
  137.7 1.5 copy.134
  139.3 41.8 %all-gather.3.cloned.1.call-done = bf16[64,4,4,2048]{3,0,2,1:T(8,128)(2,1)} async-done(((bf16[64,1,4,2048]{3,0,2,1:T(8,128)(2,1)}), bf16[64,4,4,2048]{3,0,2,1:T(8,128)(2,1)}) %all-gather.3.cloned.1.call-update) | async-done | bytes 4194320 | tf_op jit(solution)/shard_map/all_gather | solution.py:543
  181.1 6.2 %fusion.6 = f32[64,4,4,352]{3,0,2,1:T(8,128)} fusion(bf16[64,4,4,2048]{3,0,2,1:T(8,128)(2,1)} %all-gather.3.cloned.1.call-done, bf16[1,2048,352]{1,2,0:T(8,128)(2,1)} %param.31), kind=kOutput, calls=%fused_computation.17 | convolution fusion | flops 1476395008 | bytes 7077888 | tf_op jit(solution)/shard_map/slqcd,ldf->slqcf/dot_general | solution.py:544
  187.3 9.9 %convert_bitcast_fusion = bf16[64,1,4,4,2048]{4,0,3,2,1:T(8,128)(2,1)} fusion(bf16[1,352,2048]{2,1,0:T(8,128)(2,1)} %param.33, bf16[64,4,4,2048]{3,0,2,1:T(8,128)(2,1)} %all-gather.3.cloned.1.call-done, bf16[1,2048,352]{1,2,0:T(8,128)(2,1)} %param.32, f32[64,4,4,352]{3,0,2,1:T(8,128)} %fusion.6), kind=kOutput, calls=%fused_computation.5 | convolution fusion | flops 2957049856 | bytes 12713984 | tf_op jit(solution)/shard_map/slqcf,lfd->slqcd/dot_general | solution.py:549
  197.3 0.6 copy-done.17
  198.2 0.6 iota_reduce_fusion
  198.9 3.1 gather_fusion.2
  202.0 2.6 bitcast_select_fusion
  204.7 13.5 %all-to-all-start.3 = ((bf16[64,1,16,576]{3,2,1,0:T(8,128)(2,1)}), bf16[64,1,16,576]{3,2,1,0:T(8,128)(2,1)}, u32[]{:S(2)}, u32[]{:S(2)}) async-start(bf16[64,1,16,576]{3,2,1,0:T(8,128)(2,1)} %bitcast_select_fusion), calls=%async_computation.4 | async-start | bytes 2621440 | tf_op jit(solution)/shard_map/all_to_all | solution.py:538
  221.5 52.3 %reduce-scatter.2.cloned.1.call-done = bf16[64,1,1,4,2048]{4,0,3,2,1:T(8,128)(2,1)} async-done(((bf16[64,1,4,4,2048]{4,0,3,2,1:T(8,128)(2,1)}), bf16[64,1,1,4,2048]{4,0,3,2,1:T(8,128)(2,1)}) %reduce-scatter.2.cloned.1.call-update) | async-done | bytes 1048592 | tf_op jit(solution)/shard_map/reduce_scatter | solution.py:552
  273.8 3.0 copy.135
  276.8 13.9 %all-to-all-start.2 = ((bf16[64,1,1,4,2048]{4,3,2,1,0:T(4,128)(2,1)}), bf16[64,1,1,4,2048]{4,3,2,1,0:T(4,128)(2,1)}, u32[]{:S(2)}, u32[]{:S(2)}) async-start(bf16[64,1,1,4,2048]{4,3,2,1,0:T(4,128)(2,1)} %copy.135), calls=%async_computation.3 | async-start | bytes 2097152 | tf_op jit(solution)/shard_map/all_to_all | solution.py:555
  290.7 0.6 add_compare_fusion
  291.5 0.7 copy.132
  292.4 0.6 iota_reduce_fusion.1
  294.3 1.6 gather_fusion.4
  296.3 2.4 copy.136
  298.7 1.4 select_bitcast_fusion
  300.1 1.8 gather_fusion.3
  301.9 2.5 fusion.11
  304.4 17.9 %all-to-all-done.2 = bf16[64,1,1,4,2048]{4,3,2,1,0:T(4,128)(2,1)} async-done(((bf16[64,1,1,4,2048]{4,3,2,1,0:T(4,128)(2,1)}), bf16[64,1,1,4,2048]{4,3,2,1,0:T(4,128)(2,1)}, u32[]{:S(2)}, u32[]{:S(2)}) %all-to-all-start.2) | async-done | bytes 1048608 | tf_op jit(solution)/shard_map/all_to_all | solution.py:555
  322.3 1.3 reshape.461
  323.7 2.2 gather_fusion.1
  325.8 1.3 gather.33
  327.2 1.7 multiply_reduce_fusion
  328.9 0.7 add_convert_fusion
  (103 shorter events, 7.9 us)
Async XLA Ops:
  7.2 1.8 copy-start
  9.0 2.6 copy-start.1
  9.0 2.6 copy-start.9
  11.7 5.1 %copy-start.15 = (f32[512]{0:T(512)S(1)}, f32[512]{0:T(512)}, u32[]{:S(2)}) copy-start(f32[512]{0:T(512)} %param.24) | copy-start | bytes 6148
  15.4 1.5 copy-start.7
  15.4 59.8 %copy-start.5 = (bf16[2,512,128]{2,1,0:T(8,128)(2,1)S(1)}, bf16[2,512,128]{2,1,0:T(8,128)(2,1)}, u32[]{:S(2)}) copy-start(bf16[2,512,128]{2,1,0:T(8,128)(2,1)} %param.26) | copy-start | bytes 786436
  16.7 58.8 %copy-start.4 = (bf16[256,2048]{1,0:T(8,128)(2,1)S(1)}, bf16[256,2048]{1,0:T(8,128)(2,1)}, u32[]{:S(2)}) copy-start(bf16[256,2048]{1,0:T(8,128)(2,1)} %param.27) | copy-start | bytes 3145732
  75.5 5.6 %copy-start.8 = (s32[128,6]{0,1:T(8,128)S(1)}, s32[128,6]{0,1:T(8,128)}, u32[]{:S(2)}) copy-start(s32[128,6]{0,1:T(8,128)} %param.30) | copy-start | bytes 9220
  76.7 13.0 %all-to-all-start = ((bf16[4,32,2048]{2,1,0:T(8,128)(2,1)}), bf16[4,32,2048]{2,1,0:T(8,128)(2,1)}, u32[]{:S(2)}, u32[]{:S(2)}) async-start(bf16[4,32,2048]{2,1,0:T(8,128)(2,1)} %bitcast.7), calls=%async_computation | async-start | bytes 1048576 | tf_op jit(solution)/shard_map/all_to_all | solution.py:25
  81.1 100.0 %all-gather.3.cloned.1.call-start = ((), (), s32[]{:S(2)}) async-start(), calls=%async_computation.6 | async-start | bytes 5242880 | tf_op jit(solution)/shard_map/all_gather | solution.py:543
  86.0 5.9 %copy-start.11 = (s32[1,192]{1,0:T(1,128)}, s32[1,192]{1,0:T(1,128)S(1)}, u32[]{:S(2)}) copy-start(s32[1,192]{1,0:T(1,128)S(1)} %get-tuple-element.41) | copy-start | bytes 2308
  87.5 5.2 %copy-start.13 = (f32[2048]{0:T(1024)S(1)}, f32[2048]{0:T(1024)}, u32[]{:S(2)}) copy-start(f32[2048]{0:T(1024)} %param.28) | copy-start | bytes 24580
  91.9 0.7 copy-start.2
  139.3 134.6 %reduce-scatter.2.cloned.1.call-start = ((), (), s32[]{:S(2)}) async-start(), calls=%async_computation.5 | async-start | bytes 5242880 | tf_op jit(solution)/shard_map/reduce_scatter | solution.py:552
  197.2 0.7 copy-start.17
  204.7 13.5 %copy-start.14 = (s32[192]{0:T(256)S(1)}, s32[192]{0:T(256)}, u32[]{:S(2)}) copy-start(s32[192]{0:T(256)} %get-tuple-element.40) | copy-start | bytes 2308
  204.7 14.9 %copy-start.18 = (s32[256]{0:T(256)S(1)}, s32[256]{0:T(256)}, u32[]{:S(2)}) copy-start(s32[256]{0:T(256)} %param.35) | copy-start | bytes 3076
  204.7 16.3 %copy-start.12 = (s32[1,192]{1,0:T(1,128)S(1)}, s32[1,192]{1,0:T(1,128)}, u32[]{:S(2)}) copy-start(s32[1,192]{1,0:T(1,128)} %copy-done.11) | copy-start | bytes 2308
  204.7 72.2 %all-to-all-start.3 = ((bf16[64,1,16,576]{3,2,1,0:T(8,128)(2,1)}), bf16[64,1,16,576]{3,2,1,0:T(8,128)(2,1)}, u32[]{:S(2)}, u32[]{:S(2)}) async-start(bf16[64,1,16,576]{3,2,1,0:T(8,128)(2,1)} %bitcast_select_fusion), calls=%async_computation.4 | async-start | bytes 2621440 | tf_op jit(solution)/shard_map/all_to_all | solution.py:538
  276.8 15.4 %copy-start.16 = (s32[256,8]{0,1:T(8,128)S(1)}, s32[256,8]{0,1:T(8,128)}, u32[]{:S(2)}) copy-start(s32[256,8]{0,1:T(8,128)} %param.37) | copy-start | bytes 24580
  276.8 17.3 %copy-start.6 = (bf16[2048,64]{0,1:T(8,128)(2,1)S(1)}, bf16[2048,64]{0,1:T(8,128)(2,1)}, u32[]{:S(2)}) copy-start(bf16[2048,64]{0,1:T(8,128)(2,1)} %param.29) | copy-start | bytes 786436
  276.8 45.5 %all-to-all-start.2 = ((bf16[64,1,1,4,2048]{4,3,2,1,0:T(4,128)(2,1)}), bf16[64,1,1,4,2048]{4,3,2,1,0:T(4,128)(2,1)}, u32[]{:S(2)}, u32[]{:S(2)}) async-start(bf16[64,1,1,4,2048]{4,3,2,1,0:T(4,128)(2,1)} %copy.135), calls=%async_computation.3 | async-start | bytes 2097152 | tf_op jit(solution)/shard_map/all_to_all | solution.py:555
  325.8 1.4 copy-start.10
  327.2 1.8 copy-start.3
Sparse Core Ops, SparseCore 0:
  139.4 41.6 all-gather.2
  197.4 76.3 reduce-scatter.1

commit v2 on v1

--- a/solution.py
+++ b/solution.py
@@ -7,6 +7,10 @@
 from jax.sharding import PartitionSpec as P
 
 PAGE = 128
+MESH = pl.DeviceIdType.MESH
+HALF = 80
+LATW = 512
+KEYW = 640
 
 
 epsilon = 1e-06
@@ -59,25 +63,6 @@
         [rms_scale(latent[:, :latent_width], kv_gain), rotate(latent[:, latent_width:], positions)],
         axis=1,
     ).astype(jnp.bfloat16)
-
-
-def slot_table(route_ids, experts_total, capacity):
-    blocks_here = route_ids.shape[0]
-    flat_ids = route_ids.reshape(blocks_here, -1)
-    onehot = (flat_ids[:, :, None] == jnp.arange(experts_total)[None, None, :]).astype(jnp.int32)
-    row_ranks = jnp.sum((jnp.cumsum(onehot, axis=1) - 1) * onehot, axis=2)
-    return flat_ids * capacity + row_ranks
-
-
-def source_rows(target, slot_count):
-    matches = (target[:, None, :] == jnp.arange(slot_count)[None, :, None]).astype(jnp.int32)
-    return (jnp.argmax(matches, axis=2), jnp.max(matches, axis=2))
-
-
-MESH = pl.DeviceIdType.MESH
-HALF = 80
-LATW = 512
-KEYW = 640
 
 
 def remote(src, dst, send_sem, recv_sem, seq, rep):
@@ -436,6 +421,364 @@
     )(queries, own_keys)
 
 
+SLOTS = 4
+BLOCK = 32
+
+
+def expert_kernel(
+    rows_ref,
+    hidden_ref,
+    wg_hbm,
+    wu_hbm,
+    wd_hbm,
+    out_ref,
+    toks,
+    wg,
+    wu,
+    wd,
+    outb,
+    xin,
+    kept,
+    ysend,
+    yrecv,
+    back,
+    got,
+    part,
+    fsend,
+    frecv,
+    bsend,
+    brecv,
+    w_sem,
+    l_sem,
+    agf_send,
+    agf_recv,
+    agb_send,
+    agb_recv,
+    d_send,
+    d_recv,
+    s_send,
+    s_recv,
+    y_send,
+    y_recv,
+    r_send,
+    r_recv,
+    f_send,
+    f_recv,
+    b_send,
+    b_recv,
+):
+    seq = lax.axis_index("seq")
+    rep = lax.axis_index("rep")
+    core = lax.rem(rep, 2)
+    zc = lax.rem(seq // 4, 4) * 2 + rep // 2
+    zhi = lax.rem(seq // 4, 4)
+    x0 = seq // 16
+    y0 = lax.rem(seq, 4)
+    here = x0 * 4 + y0
+    way = 1 - 2 * core
+    mate = rep + 1 - 2 * core
+    width = hidden_ref.shape[1]
+
+    def chip(z):
+        z = lax.rem(z + 8, 8)
+        return x0 * 16 + (z // 2) * 4 + y0, lax.rem(z, 2) * 2 + core
+
+    ahead = chip(zc + way)
+    behind = chip(zc - way)
+
+    def to_peer(p):
+        return lax.rem(x0 + p // 4, 4), lax.rem(y0 + lax.rem(p, 4), 4)
+
+    def from_peer(p):
+        return lax.rem(x0 + 4 - p // 4, 4), lax.rem(y0 + 4 - lax.rem(p, 4), 4)
+
+    def plane_seq(xy):
+        return xy[0] * 16 + zhi * 4 + xy[1]
+
+    partners = [ahead, behind, (seq, mate)] + [(plane_seq(to_peer(p)), rep) for p in range(1, 16)]
+
+    w_copies = [
+        pltpu.make_async_copy(wg_hbm.at[0], wg, w_sem.at[0]),
+        pltpu.make_async_copy(wu_hbm.at[0], wu, w_sem.at[1]),
+        pltpu.make_async_copy(wd_hbm.at[0], wd, w_sem.at[2]),
+    ]
+    for copy in w_copies:
+        copy.start()
+    first = pltpu.make_async_copy(rows_ref, toks.at[0], l_sem.at[0])
+    first.start()
+    first.wait()
+    greet(partners)
+
+    def agf(k):
+        source = (0, 1, 3, 5)[k]
+        return remote(
+            toks.at[source], toks.at[2 * k + 1], agf_send.at[k], agf_recv.at[k], ahead[0], ahead[1]
+        )
+
+    def agb(k):
+        source = (0, 2, 4)[k]
+        return remote(
+            toks.at[source], toks.at[2 * k + 2], agb_send.at[k], agb_recv.at[k], behind[0], behind[1]
+        )
+
+    lane = lax.broadcasted_iota(jnp.int32, (1, 256), 1)
+    code = (
+        (((lane >> 6) * 16) + zhi * 4 + ((lane >> 4) & 3)) * SLOTS + (lane & 3)
+    ).astype(jnp.float32)
+    lane_block = (lane >> 2) & 3
+    token_block = lax.broadcasted_iota(jnp.int32, (128, 1), 0) >> 5
+    same_block = token_block == lane_block
+
+    def tokens_of(ph):
+        return toks[4 * ph : 4 * ph + 4].reshape(128, width + 128)
+
+    def dispatch_copy(ph, p):
+        xy = to_peer(p)
+        return remote(
+            outb.at[ph, xy[0] * 4 + xy[1]],
+            xin.at[core, ph, here],
+            d_send.at[ph, p],
+            d_recv.at[ph, p],
+            plane_seq(xy),
+            rep,
+        )
+
+    def own_rows(ph):
+        return pltpu.make_async_copy(
+            outb.at[ph, here], xin.at[core, ph, here], l_sem.at[1 + ph]
+        )
+
+    def share(ph, p):
+        xy = from_peer(p)
+        slot = xin.at[core, ph, xy[0] * 4 + xy[1]]
+        return remote(slot, slot, s_send.at[ph, p], s_recv.at[ph, p], seq, mate)
+
+    def share_arrival(ph, p):
+        xy = from_peer(p)
+        slot = xin.at[1 - core, ph, xy[0] * 4 + xy[1]]
+        return remote(slot, slot, s_send.at[ph, p], s_recv.at[ph, p], seq, mate)
+
+    def dispatch(ph):
+        block = tokens_of(ph)
+        meta = block[:, width:].astype(jnp.float32)
+        hit = meta[:, 0:1] == code
+        for k in range(1, 6):
+            hit = hit | (meta[:, k : k + 1] == code)
+        pick = jnp.where(hit & same_block, 1.0, 0.0).astype(jnp.bfloat16)
+        rows = lax.dot_general(
+            pick, block[:, :width], (((0,), (0,)), ((), ())), preferred_element_type=jnp.float32
+        )
+        outb[ph] = rows.astype(jnp.bfloat16).reshape(16, 16, width)
+
+        def send(p, carry):
+            dispatch_copy(ph, p).start()
+            return carry
+
+        lax.fori_loop(1, 16, send, 0)
+        own_rows(ph).start()
+
+    def arrivals(ph):
+        own_rows(ph).wait()
+        share(ph, 0).start()
+
+        def one(p, carry):
+            dispatch_copy(ph, p).wait_recv()
+            share(ph, p).start()
+            return carry
+
+        lax.fori_loop(1, 16, one, 0)
+
+    def share_arrivals(ph):
+        def one(p, carry):
+            share_arrival(ph, p).wait_recv()
+            return carry
+
+        lax.fori_loop(0, 16, one, 0)
+
+    def expert(which, ph):
+        rows = xin[which, ph].reshape(256, width)
+        gate = jnp.dot(rows, wg[...], preferred_element_type=jnp.float32)
+        up = jnp.dot(rows, wu[...], preferred_element_type=jnp.float32)
+        act = (jax.nn.silu(gate) * up).astype(jnp.bfloat16)
+        return jnp.dot(act, wd[...], preferred_element_type=jnp.float32)
+
+    def pair_copy(ph):
+        return remote(ysend.at[ph], yrecv.at[ph], y_send.at[ph], y_recv.at[ph], seq, mate)
+
+    def return_copy(ph, p):
+        xy = to_peer(p)
+        return remote(
+            back.at[ph, xy[0] * 4 + xy[1]],
+            got.at[ph, here],
+            r_send.at[ph, p],
+            r_recv.at[ph, p],
+            plane_seq(xy),
+            rep,
+        )
+
+    def own_back(ph):
+        return pltpu.make_async_copy(back.at[ph, here], got.at[ph, here], l_sem.at[3 + ph])
+
+    def give_back(ph):
+        pair_copy(ph).wait_recv()
+        total = kept[ph] + yrecv[ph].astype(jnp.float32)
+        back[ph] = total.astype(jnp.bfloat16).reshape(16, 16, width)
+
+        def send(p, carry):
+            return_copy(ph, p).start()
+            return carry
+
+        lax.fori_loop(1, 16, send, 0)
+        own_back(ph).start()
+
+    def combine(ph):
+        def one(p, carry):
+            return_copy(ph, p).wait_recv()
+            return carry
+
+        lax.fori_loop(1, 16, one, 0)
+        own_back(ph).wait()
+        meta = toks[4 * ph : 4 * ph + 4, :, width:].reshape(128, 128).astype(jnp.float32)
+        high = jnp.zeros((128, 256), jnp.float32)
+        low = jnp.zeros((128, 256), jnp.float32)
+        for k in range(6):
+            hit = (meta[:, k : k + 1] == code) & same_block
+            high = high + jnp.where(hit, meta[:, 6 + k : 7 + k], 0.0)
+            low = low + jnp.where(hit, meta[:, 12 + k : 13 + k], 0.0)
+        both = jnp.concatenate([high, low], axis=0).astype(jnp.bfloat16)
+        sums = jnp.dot(both, got[ph].reshape(256, width), preferred_element_type=jnp.float32)
+        part[4 * ph : 4 * ph + 4] = (sums[:128] + sums[128:]).reshape(4, BLOCK, width)
+
+    agf(0).start()
+    agb(0).start()
+    agf(0).wait_recv()
+    agf(1).start()
+    agb(0).wait_recv()
+    agb(1).start()
+    agf(1).wait_recv()
+    agf(2).start()
+    dispatch(0)
+    agb(1).wait_recv()
+    agb(2).start()
+    agf(2).wait_recv()
+    agf(3).start()
+    agb(2).wait_recv()
+    agf(3).wait_recv()
+    dispatch(1)
+    for copy in w_copies:
+        copy.wait()
+    arrivals(0)
+    kept[0] = expert(core, 0)
+    share_arrivals(0)
+    ysend[0] = expert(1 - core, 0).astype(jnp.bfloat16)
+    pair_copy(0).start()
+    arrivals(1)
+    kept[1] = expert(core, 1)
+    give_back(0)
+    share_arrivals(1)
+    ysend[1] = expert(1 - core, 1).astype(jnp.bfloat16)
+    pair_copy(1).start()
+    give_back(1)
+    combine(0)
+    combine(1)
+
+    def f_copy(k):
+        return remote(fsend.at[k], frecv.at[k], f_send.at[k], f_recv.at[k], ahead[0], ahead[1])
+
+    def b_copy(k):
+        return remote(bsend.at[k], brecv.at[k], b_send.at[k], b_recv.at[k], behind[0], behind[1])
+
+    fsend[0] = part[7].astype(jnp.bfloat16)
+    f_copy(0).start()
+    bsend[0] = part[5].astype(jnp.bfloat16)
+    b_copy(0).start()
+    for k in range(1, 4):
+        f_copy(k - 1).wait_recv()
+        fsend[k] = (part[(7, 6, 4, 2)[k]] + frecv[k - 1].astype(jnp.float32)).astype(jnp.bfloat16)
+        f_copy(k).start()
+        if k < 3:
+            b_copy(k - 1).wait_recv()
+            bsend[k] = (part[(5, 3, 1)[k]] + brecv[k - 1].astype(jnp.float32)).astype(jnp.bfloat16)
+            b_copy(k).start()
+    b_copy(2).wait_recv()
+    total = hidden_ref[...] + part[0] + brecv[2].astype(jnp.float32)
+    f_copy(3).wait_recv()
+    out_ref[...] = (total + frecv[3].astype(jnp.float32)).astype(out_ref.dtype)
+
+    for k in range(4):
+        agf(k).wait_send()
+        f_copy(k).wait_send()
+    for k in range(3):
+        agb(k).wait_send()
+        b_copy(k).wait_send()
+    for ph in range(2):
+        pair_copy(ph).wait_send()
+        share(ph, 0).wait_send()
+
+        def drain(p, carry):
+            dispatch_copy(ph, p).wait_send()
+            share(ph, p).wait_send()
+            return_copy(ph, p).wait_send()
+            return carry
+
+        lax.fori_loop(1, 16, drain, 0)
+
+
+def expert_layer(rows, hidden, w_gate, w_up, w_down):
+    width = hidden.shape[1]
+    hidden_units = w_gate.shape[2]
+    dma = pltpu.SemaphoreType.DMA
+    bf16 = jnp.bfloat16
+    vmem = pl.BlockSpec(memory_space=pltpu.VMEM)
+    anywhere = pl.BlockSpec(memory_space=pl.ANY)
+    return pl.pallas_call(
+        expert_kernel,
+        out_shape=jax.ShapeDtypeStruct(hidden.shape, bf16),
+        in_specs=[vmem, vmem, anywhere, anywhere, anywhere],
+        out_specs=vmem,
+        scratch_shapes=[
+            pltpu.VMEM((8, BLOCK, width + 128), bf16),
+            pltpu.VMEM((width, hidden_units), bf16),
+            pltpu.VMEM((width, hidden_units), bf16),
+            pltpu.VMEM((hidden_units, width), bf16),
+            pltpu.VMEM((2, 16, 16, width), bf16),
+            pltpu.VMEM((2, 2, 16, 16, width), bf16),
+            pltpu.VMEM((2, 256, width), jnp.float32),
+            pltpu.VMEM((2, 256, width), bf16),
+            pltpu.VMEM((2, 256, width), bf16),
+            pltpu.VMEM((2, 16, 16, width), bf16),
+            pltpu.VMEM((2, 16, 16, width), bf16),
+            pltpu.VMEM((8, BLOCK, width), jnp.float32),
+            pltpu.VMEM((4, BLOCK, width), bf16),
+            pltpu.VMEM((4, BLOCK, width), bf16),
+            pltpu.VMEM((3, BLOCK, width), bf16),
+            pltpu.VMEM((3, BLOCK, width), bf16),
+            dma((3,)),
+            dma((5,)),
+            dma((4,)),
+            dma((4,)),
+            dma((3,)),
+            dma((3,)),
+            dma((2, 16)),
+            dma((2, 16)),
+            dma((2, 16)),
+            dma((2, 16)),
+            dma((2,)),
+            dma((2,)),
+            dma((2, 16)),
+            dma((2, 16)),
+            dma((4,)),
+            dma((4,)),
+            dma((3,)),
+            dma((3,)),
+        ],
+        name="experts",
+        compiler_params=pltpu.CompilerParams(
+            collective_id=1, has_side_effects=True, vmem_limit_bytes=56 << 20
+        ),
+    )(rows, hidden, w_gate, w_up, w_down)
+
+
 def on_device(
     tokens,
     prior_cache,
@@ -502,23 +845,37 @@
         .reshape(tok_dev, -1)
     )
     head_partial = jnp.dot(heads_out, out_weight, preferred_element_type=jnp.float32)
-    experts_total = router.shape[1]
-    local_experts = w_gate.shape[0]
     top_count = expert_ids.shape[1]
-    capacity = max(2, min(quarter, 4 * quarter * top_count // (3 * experts_total)))
-    slot_count = experts_total * capacity
-    target = slot_table(expert_ids.reshape(rep_count, quarter, top_count), experts_total, capacity)
-    own_target = lax.dynamic_index_in_dim(target, rep_index, 0, keepdims=False)
-    model_width = tokens.shape[1]
+    own_ids = lax.dynamic_slice_in_dim(expert_ids, rep_index * quarter, quarter, 0)
+    flat_ids = own_ids.reshape(-1)
+    flat_index = jnp.arange(flat_ids.shape[0])
+    rank = jnp.sum(
+        (
+            (flat_ids[:, None] == flat_ids[None, :]) & (flat_index[None, :] < flat_index[:, None])
+        ).astype(jnp.int32),
+        axis=1,
+    )
+    target = (flat_ids * SLOTS + rank).reshape(quarter, top_count)
     attention = sent_and_summed(head_partial.astype(jnp.bfloat16), "rep", 0)
     hidden_own = lax.dynamic_slice_in_dim(token_float, rep_index * quarter, quarter, 0) + attention
     moe_own = rms_scale(hidden_own, moe_gain).astype(jnp.bfloat16)
-    rows_from, live_mask = source_rows(own_target[None, :], slot_count)
-    token_of = (rows_from // top_count).reshape(1, experts_total, capacity).transpose(1, 0, 2)
-    live_mask = live_mask.reshape(1, experts_total, capacity).transpose(1, 0, 2)
-    outgoing = jnp.where(
-        live_mask[..., None] > 0, jnp.take(moe_own, token_of, axis=0), jnp.zeros((), jnp.bfloat16)
-    )
+    logits = jnp.dot(moe_own, router, preferred_element_type=jnp.float32)
+    named = own_ids[:, :, None] == jnp.arange(router.shape[1])[None, None, :]
+    chosen = jnp.sum(jnp.where(named, logits[:, None, :], 0.0), axis=2)
+    gate_score = jax.nn.sigmoid(chosen)
+    weights = route_scale * gate_score / jnp.sum(gate_score, axis=1, keepdims=True)
+    high = lax.reduce_precision(weights, 8, 7)
+    sent_rows = jnp.concatenate(
+        [
+            moe_own,
+            target.astype(jnp.bfloat16),
+            high.astype(jnp.bfloat16),
+            (weights - high).astype(jnp.bfloat16),
+            jnp.zeros((quarter, 128 - 3 * top_count), jnp.bfloat16),
+        ],
+        axis=1,
+    )
+    layer_out = expert_layer(sent_rows, hidden_own, w_gate, w_up, w_down)
     group_size = handover.shape[0]
     req_dev = group_size // seq_count
     owner_here = lax.dynamic_slice_in_dim(request_owner, rep_index * group_size, group_size, 0)
@@ -533,36 +890,7 @@
     order_key = owner_here * req_dev + earlier
     picked = jnp.argmax((order_key[None, :] == request_index[:, None]).astype(jnp.int32), axis=1)
     parcel = jnp.take(handover, picked, axis=0)
-    arrived, parcels = (
-        lax.all_to_all(outgoing, "seq", split_axis=0, concat_axis=0, tiled=True),
-        lax.all_to_all(parcel, "seq", split_axis=0, concat_axis=0, tiled=True),
-    )
-    expert_rows = arrived.reshape(
-        seq_count, local_experts, outgoing.shape[1], capacity, model_width
-    )
-    expert_rows = lax.all_gather(expert_rows, "rep", axis=2, tiled=True)
-    gate_sum = jnp.einsum(
-        "slqcd,ldf->slqcf", expert_rows, w_gate, preferred_element_type=jnp.float32
-    )
-    up_sum = jnp.einsum("slqcd,ldf->slqcf", expert_rows, w_up, preferred_element_type=jnp.float32)
-    activated = (jax.nn.silu(gate_sum) * up_sum).astype(jnp.bfloat16)
-    expert_out = jnp.einsum(
-        "slqcf,lfd->slqcd", activated, w_down, preferred_element_type=jnp.float32
-    )
-    expert_share = lax.psum_scatter(
-        expert_out.astype(jnp.bfloat16), "rep", scatter_dimension=2, tiled=True
-    )
-    returned = lax.all_to_all(expert_share, "seq", split_axis=0, concat_axis=0, tiled=True).reshape(
-        slot_count, model_width
-    )
-    own_ids = lax.dynamic_slice_in_dim(expert_ids, rep_index * quarter, quarter, 0)
-    logits = jnp.dot(moe_own, router, preferred_element_type=jnp.float32)
-    chosen = jnp.take_along_axis(logits, own_ids, axis=1)
-    gate_score = jax.nn.sigmoid(chosen)
-    weights = route_scale * gate_score / jnp.sum(gate_score, axis=1, keepdims=True)
-    gathered = jnp.take(returned, own_target, axis=0).reshape(quarter, top_count, model_width)
-    moe_sum = jnp.sum(weights[..., None] * gathered.astype(jnp.float32), axis=1)
-    layer_out = (hidden_own + moe_sum).astype(jnp.bfloat16)
+    parcels = lax.all_to_all(parcel, "seq", split_axis=0, concat_axis=0, tiled=True)
     layers_here = handover.shape[1]
     pos_dev = handover.shape[2]
     row_width = handover.shape[3]

time: 337 us -> 222 us (0.66)
  waiting for transfers between devices: 112 us -> 0.01 us
  Pallas kernels: 58.3 us -> 164 us
  blocking collectives: 40.5 us -> 0 us
  starting transfers between devices: 31.8 us -> 13.2 us
  matrix products: 23.3 us -> 6.14 us
  between operations: 15.8 us -> 2.37 us
  local copies, waits for them, and re-layouts: 28.4 us -> 17.2 us
  other arithmetic: 26.5 us -> 16.6 us
    pallas_call x0 -> x1, Pallas kernels: none -> 106 us  [expert_layer(): pl.pallas_call(expert_kernel, out_shape=jax.ShapeDtypeStruct(hidden.shape...]
    reduce_scatter x1 -> x0, waiting for transfers between devices: 52.3 us -> none  [on_device(): lax.psum_scatter(expert_out.astype(jnp.bfloat16), 'rep', scatter_dimensio...]
    all_gather x1 -> x0, waiting for transfers between devices: 41.8 us -> none  [on_device(): expert_rows = lax.all_gather(expert_rows, 'rep', axis=2, tiled=True)]
    all_to_all x1 -> x0, blocking collectives: 40.5 us -> none  [on_device(): lax.all_to_all(outgoing, 'seq', split_axis=0, concat_axis=0, tiled=True)]
    all_to_all x1 -> x0, waiting for transfers between devices: 17.9 us -> none  [on_device(): lax.all_to_all(expert_share, 'seq', split_axis=0, concat_axis=0, tiled=True)]
    dot_general x2 -> x0, matrix products: 16.1 us -> none  [the longest x1 9.93 us: on_device(): jnp.einsum('slqcf,lfd->slqcd', activated, w_down, preferred_element_type=...]
    all_to_all x1 -> x0, starting transfers between devices: 13.9 us -> none  [on_device(): lax.all_to_all(expert_share, 'seq', split_axis=0, concat_axis=0, tiled=True)]
    gather x9 -> x0, local copies, waits for them, and re-layouts: 8.06 us -> none  [the longest x2 3.5 us: on_device(): jnp.take(returned, own_target, axis=0)]
  transfers between devices with their start and end apart: 5 -> 2, of which waited for: 3 -> 0; matrix products, arithmetic and copies ran while one was open for 10% -> 8% of each run, Pallas kernels for 0% -> 48%
where the time goes in v2:
time: 222 us; the launch traced here: 220 us
  Pallas kernels  164 us (74%)
  local copies, waits for them, and re-layouts  17.2 us (8%)
  other arithmetic  16.6 us (7%)
  starting transfers between devices  13.2 us (6%)
  matrix products  6.14 us (3%)
  between operations  2.37 us (1%)
    pallas_call x1, Pallas kernels, expert_layer(): pl.pallas_call(expert_kernel, out_shape=jax.ShapeDtypeStruct(hidden.shape...  106 us
    pallas_call x1, Pallas kernels, gathered_attention(): pl.pallas_call(functools.partial(attend_kernel, scale, prior_rows, span_r...  58.2 us
    all_to_all x1, starting transfers between devices, on_device(): lax.all_to_all(parcel, 'seq', split_axis=0, concat_axis=0, tiled=True)  9.49 us
    unnamed x38, local copies, waits for them, and re-layouts  5.97 us
  transfers between devices with their start and end apart: 2, of which 0 were waited for; matrix products, arithmetic and copies ran while one was open for 8% of the time, Pallas kernels for 48%

profile of v2, /device:TPU:32, one launch (start us, length us, event | category | flops | bytes accessed | tf_op | source)
XLA Modules:
  0.0 219.9 jit_solution(11940986540488755357)
XLA Ops:
  0.7 1.4 multiply_reduce_fusion
  2.1 2.4 %fusion.13 = f32[128,384]{0,1:T(8,128)S(1)} fusion(bf16[2048,384]{1,0:T(8,128)(2,1)} %param.22, f32[2048]{0:T(1024)} %param.21, f32[128]{0:T(128)S(1)} %add_rsqrt_fusion.2, bf16[128,2048]{1,0:T(8,128)(2,1)} %param.19), kind=kOutput, calls=%fused_computation.33 | convolution fusion | flops 202375168 | bytes 2302464 | tf_op jit(solution)/shard_map/dot_general | solution.py:819
  4.5 0.9 fusion.12
  5.5 0.7 multiply_reduce_fusion.2
  6.2 0.9 subtract_convert_fusion
  7.2 0.7 copy.91
  7.9 0.7 subtract_convert_fusion.1
  8.6 0.6 maximum_bitcast_fusion
  9.2 0.9 copy.93
  10.1 1.2 convolution_convert_fusion.1
  11.4 0.7 add_rsqrt_fusion.1
  12.1 0.1 multiply_convert_fusion.2
  12.3 0.1 fusion.8.own_ref
  12.4 58.2 %gather_attend.1 = bf16[256,512]{1,0:T(8,128)(2,1)S(1)} custom-call(bf16[256,640]{1,0:T(8,128)(2,1)S(1)} %fusion.7.q_ref, bf16[160,640]{1,0:T(8,128)(2,1)S(1)} %fusion.8.own_ref), custom_call_target="tpu_custom_call" | custom-call | tf_op jit(solution)/shard_map/gather_attend/pallas_call | solution.py:392
  70.6 0.3 convolution_convert_fusion.2
  71.0 1.1 convolution_convert_fusion
  72.1 3.8 %all-to-all-start = ((bf16[4,32,2048]{2,1,0:T(8,128)(2,1)}), bf16[4,32,2048]{2,1,0:T(8,128)(2,1)S(1)}, u32[]{:S(2)}, u32[]{:S(2)}) async-start(bf16[4,32,2048]{2,1,0:T(8,128)(2,1)} %bitcast.7), calls=%async_computation | async-start | bytes 1048576 | tf_op jit(solution)/shard_map/all_to_all | solution.py:29
  75.9 0.2 convert_reduce_fusion.2
  76.1 0.1 dynamic-slice_add_fusion.2
  76.2 0.7 iota_reduce_fusion
  77.0 0.1 copy.111
  77.1 0.1 eq.17
  77.2 0.2 convert_reduce_fusion.1
  77.4 0.7 dynamic_slice.15
  78.8 0.2 fusion.16
  79.0 0.7 iota_reduce_fusion.1
  79.7 0.6 dynamic-slice.6
  80.3 3.1 %gather_fusion = bf16[64,16,576]{2,1,0:T(8,128)(2,1)} fusion(bf16[64,16,576]{2,1,0:T(8,128)(2,1)} %bitcast.36, s32[1024]{0:T(1024)S(1)} %pad_clamp_fusion.1), kind=kCustom, calls=%fused_computation | custom fusion | bytes 2359552 | tf_op jit(solution)/shard_map/jit(_take)/gather | solution.py:892
  84.0 2.6 %bitcast_select_fusion = bf16[64,1,16,576]{3,2,1,0:T(8,128)(2,1)} fusion(bf16[64,16,576]{2,1,0:T(8,128)(2,1)} %gather_fusion, pred[64]{0:T(512)(128)(4,1)S(1)} %compare_and_fusion), kind=kLoop, calls=%fused_computation.3 | loop fusion | flops 589824 | bytes 2359360 | tf_op jit(solution)/shard_map/jit(_take)/select_n | solution.py:892
  86.6 9.5 %all-to-all-start.1 = ((bf16[64,1,16,576]{3,2,1,0:T(8,128)(2,1)}), bf16[64,1,16,576]{3,2,1,0:T(8,128)(2,1)}, u32[]{:S(2)}, u32[]{:S(2)}) async-start(bf16[64,1,16,576]{3,2,1,0:T(8,128)(2,1)} %bitcast_select_fusion), calls=%async_computation.1 | async-start | bytes 2621440 | tf_op jit(solution)/shard_map/all_to_all | solution.py:893
  96.1 1.1 convert_element_type.74
  97.2 0.1 reduce_sum.79
  97.3 2.6 %copy.103.wg_hbm = bf16[1,2048,352]{2,1,0:T(8,128)(2,1)} copy(bf16[1,2048,352]{1,2,0:T(8,128)(2,1)} %param.31) | data formatting | bytes 2883584 | tf_op args[12]
  99.9 2.6 %copy.104.wu_hbm = bf16[1,2048,352]{2,1,0:T(8,128)(2,1)} copy(bf16[1,2048,352]{1,2,0:T(8,128)(2,1)} %param.32) | data formatting | bytes 2883584 | tf_op args[13]
  102.5 1.1 multiply_reduce_fusion.1
  103.7 0.1 multiply_convert_fusion.1
  103.8 0.2 fusion.18
  104.0 0.2 select_reduce_fusion
  104.2 0.1 copy.100
  104.2 0.1 fusion.17
  104.4 0.1 fusion.15
  104.5 0.8 concatenate.29.rows_ref
  105.3 106.0 %experts.1 = bf16[32,2048]{1,0:T(8,128)(2,1)} custom-call(bf16[32,2176]{1,0:T(8,128)(2,1)} %concatenate.29.rows_ref, f32[32,2048]{1,0:T(8,128)} %copy-done.2, bf16[1,2048,352]{2,1,0:T(8,128)(2,1)} %copy.103.wg_hbm, bf16[1,2048,352]{2,1,0:T(8,128)(2,1)} %copy.104.wu_hbm, bf16[1,352,2048]{2,1,0:T(8,128)(2,1)} %wd_hbm.1), custom_call_target="tpu_custom_call" | custom-call | tf_op jit(solution)/shard_map/experts/pallas_call | solution.py:734
  211.3 2.4 %copy.105 = bf16[8,1,128,576]{2,3,0,1:T(8,128)(2,1)} copy(bf16[8,1,128,576]{3,2,0,1:T(8,128)(2,1)} %bitcast.14) | data formatting | bytes 2359296 | tf_op jit(solution)/shard_map/reshape;transpose;reshape | solution.py:902
  213.7 1.4 select_bitcast_fusion
  215.1 1.7 gather_fusion.1
  216.8 2.5 %fusion = bf16[8,1,128,576]{2,3,1,0:T(8,128)(2,1)} fusion(bf16[8,128,576]{1,2,0:T(8,128)(2,1)} %gather_fusion.1, pred[8]{0:T(512)(128)(4,1)S(1)} %compare_and_fusion.1), kind=kLoop, calls=%fused_computation.6 | loop fusion | flops 589824 | bytes 2359304
  219.3 0.7 copy.113
  (55 shorter events, 0.5 us)
Async XLA Ops:
  0.6 3.8 %copy-start = (bf16[2048,576]{0,1:T(8,128)(2,1)S(1)}, bf16[2048,576]{0,1:T(8,128)(2,1)}, u32[]{:S(2)}) copy-start(bf16[2048,576]{0,1:T(8,128)(2,1)} %param.23) | copy-start | bytes 7077892
  0.7 3.8 %copy-start.1 = (bf16[128,2048]{1,0:T(8,128)(2,1)S(1)}, bf16[128,2048]{1,0:T(8,128)(2,1)}, u32[]{:S(2)}) copy-start(bf16[128,2048]{1,0:T(8,128)(2,1)} %param.19) | copy-start | bytes 1572868
  0.7 3.8 %copy-start.10 = (f32[2048]{0:T(1024)S(1)}, f32[2048]{0:T(1024)}, u32[]{:S(2)}) copy-start(f32[2048]{0:T(1024)} %param.21) | copy-start | bytes 24580
  7.2 5.1 %copy-start.7 = (bf16[128,32]{1,0:T(8,128)(2,1)S(1)}, bf16[128,32]{1,0:T(8,128)(2,1)}, u32[]{:S(2)}) copy-start(bf16[128,32]{1,0:T(8,128)(2,1)} %get-tuple-element.42) | copy-start | bytes 24580
  7.2 5.1 %copy-start.8 = (bf16[128,32]{1,0:T(8,128)(2,1)S(1)}, bf16[128,32]{1,0:T(8,128)(2,1)}, u32[]{:S(2)}) copy-start(bf16[128,32]{1,0:T(8,128)(2,1)} %get-tuple-element.43) | copy-start | bytes 24580
  8.6 3.5 %copy-start.13 = (f32[512]{0:T(512)S(1)}, f32[512]{0:T(512)}, u32[]{:S(2)}) copy-start(f32[512]{0:T(512)} %param.24) | copy-start | bytes 6148
  10.1 2.2 copy-start.9
  11.4 59.3 %copy-start.5 = (bf16[2,512,128]{2,1,0:T(8,128)(2,1)S(1)}, bf16[2,512,128]{2,1,0:T(8,128)(2,1)}, u32[]{:S(2)}) copy-start(bf16[2,512,128]{2,1,0:T(8,128)(2,1)} %param.26) | copy-start | bytes 786436
  12.1 58.8 %copy-start.3 = (bf16[256,2048]{1,0:T(8,128)(2,1)S(1)}, bf16[256,2048]{1,0:T(8,128)(2,1)}, u32[]{:S(2)}) copy-start(bf16[256,2048]{1,0:T(8,128)(2,1)} %param.27) | copy-start | bytes 3145732
  70.9 4.9 %copy-start.15 = (s32[256]{0:T(256)S(1)}, s32[256]{0:T(256)}, u32[]{:S(2)}) copy-start(s32[256]{0:T(256)} %param.36) | copy-start | bytes 3076
  70.9 6.0 %copy-start.12 = (s32[128,6]{0,1:T(8,128)S(1)}, s32[128,6]{0,1:T(8,128)}, u32[]{:S(2)}) copy-start(s32[128,6]{0,1:T(8,128)} %param.30) | copy-start | bytes 9220
  70.9 7.8 %copy-start.14 = (s32[256,8]{0,1:T(8,128)S(1)}, s32[256,8]{0,1:T(8,128)}, u32[]{:S(2)}) copy-start(s32[256,8]{0,1:T(8,128)} %param.37) | copy-start | bytes 24580
  70.9 8.7 %copy-start.16 = (s32[256]{0:T(256)S(1)}, s32[256]{0:T(256)}, u32[]{:S(2)}) copy-start(s32[256]{0:T(256)} %param.35) | copy-start | bytes 3076
  72.1 14.5 %all-to-all-start = ((bf16[4,32,2048]{2,1,0:T(8,128)(2,1)}), bf16[4,32,2048]{2,1,0:T(8,128)(2,1)S(1)}, u32[]{:S(2)}, u32[]{:S(2)}) async-start(bf16[4,32,2048]{2,1,0:T(8,128)(2,1)} %bitcast.7), calls=%async_computation | async-start | bytes 1048576 | tf_op jit(solution)/shard_map/all_to_all | solution.py:29
  86.6 124.7 %all-to-all-start.1 = ((bf16[64,1,16,576]{3,2,1,0:T(8,128)(2,1)}), bf16[64,1,16,576]{3,2,1,0:T(8,128)(2,1)}, u32[]{:S(2)}, u32[]{:S(2)}) async-start(bf16[64,1,16,576]{3,2,1,0:T(8,128)(2,1)} %bitcast_select_fusion), calls=%async_computation.1 | async-start | bytes 2621440 | tf_op jit(solution)/shard_map/all_to_all | solution.py:893
  102.4 1.2 copy-start.11
  102.4 1.3 copy-start.6
  103.6 1.6 copy-start.2
  216.8 2.5 %copy-start.4 = (bf16[32,2048]{1,0:T(8,128)(2,1)S(1)}, bf16[32,2048]{1,0:T(8,128)(2,1)}, u32[]{:S(2)}) copy-start(bf16[32,2048]{1,0:T(8,128)(2,1)} %experts.1) | copy-start | bytes 393220

commit v3 on v2

--- a/solution.py
+++ b/solution.py
@@ -597,8 +597,9 @@
 
     def expert(which, ph):
         rows = xin[which, ph].reshape(256, width)
-        gate = jnp.dot(rows, wg[...], preferred_element_type=jnp.float32)
-        up = jnp.dot(rows, wu[...], preferred_element_type=jnp.float32)
+        across = (((1,), (1,)), ((), ()))
+        gate = lax.dot_general(rows, wg[...], across, preferred_element_type=jnp.float32)
+        up = lax.dot_general(rows, wu[...], across, preferred_element_type=jnp.float32)
         act = (jax.nn.silu(gate) * up).astype(jnp.bfloat16)
         return jnp.dot(act, wd[...], preferred_element_type=jnp.float32)
 
@@ -726,7 +727,7 @@
 
 def expert_layer(rows, hidden, w_gate, w_up, w_down):
     width = hidden.shape[1]
-    hidden_units = w_gate.shape[2]
+    hidden_units = w_gate.shape[1]
     dma = pltpu.SemaphoreType.DMA
     bf16 = jnp.bfloat16
     vmem = pl.BlockSpec(memory_space=pltpu.VMEM)
@@ -738,8 +739,8 @@
         out_specs=vmem,
         scratch_shapes=[
             pltpu.VMEM((8, BLOCK, width + 128), bf16),
-            pltpu.VMEM((width, hidden_units), bf16),
-            pltpu.VMEM((width, hidden_units), bf16),
+            pltpu.VMEM((hidden_units, width), bf16),
+            pltpu.VMEM((hidden_units, width), bf16),
             pltpu.VMEM((hidden_units, width), bf16),
             pltpu.VMEM((2, 16, 16, width), bf16),
             pltpu.VMEM((2, 2, 16, 16, width), bf16),
@@ -857,7 +858,8 @@
     )
     target = (flat_ids * SLOTS + rank).reshape(quarter, top_count)
     attention = sent_and_summed(head_partial.astype(jnp.bfloat16), "rep", 0)
-    hidden_own = lax.dynamic_slice_in_dim(token_float, rep_index * quarter, quarter, 0) + attention
+    own_tokens = lax.dynamic_slice_in_dim(tokens, rep_index * quarter, quarter, 0)
+    hidden_own = own_tokens.astype(jnp.float32) + attention
     moe_own = rms_scale(hidden_own, moe_gain).astype(jnp.bfloat16)
     logits = jnp.dot(moe_own, router, preferred_element_type=jnp.float32)
     named = own_ids[:, :, None] == jnp.arange(router.shape[1])[None, None, :]
@@ -875,7 +877,9 @@
         ],
         axis=1,
     )
-    layer_out = expert_layer(sent_rows, hidden_own, w_gate, w_up, w_down)
+    layer_out = expert_layer(
+        sent_rows, hidden_own, jnp.swapaxes(w_gate, 1, 2), jnp.swapaxes(w_up, 1, 2), w_down
+    )
     group_size = handover.shape[0]
     req_dev = group_size // seq_count
     owner_here = lax.dynamic_slice_in_dim(request_owner, rep_index * group_size, group_size, 0)
@@ -889,7 +893,7 @@
     )
     order_key = owner_here * req_dev + earlier
     picked = jnp.argmax((order_key[None, :] == request_index[:, None]).astype(jnp.int32), axis=1)
-    parcel = jnp.take(handover, picked, axis=0)
+    parcel = handover.at[picked].get(mode="promise_in_bounds")
     parcels = lax.all_to_all(parcel, "seq", split_axis=0, concat_axis=0, tiled=True)
     layers_here = handover.shape[1]
     pos_dev = handover.shape[2]
@@ -904,19 +908,24 @@
     own_requests = (
         lax.dynamic_slice_in_dim(picked, seq_index * req_dev, req_dev, 0) + rep_index * group_size
     )
-    own_lengths = jnp.take(lengths, own_requests)
-    alive_mask = jnp.arange(maxlen)[None, :] < own_lengths[:, None]
-    stacked = jnp.where(alive_mask[:, None, :, None], stacked, jnp.zeros((), jnp.bfloat16))
+    own_lengths = lengths.at[own_requests].get(mode="promise_in_bounds")
     page_rows = (
         stacked.reshape(req_dev, layers_here, pages_per, PAGE, row_width)
         .transpose(0, 2, 1, 3, 4)
         .reshape(req_dev * pages_per, layers_here, PAGE, row_width)
     )
-    physical = jnp.take(page_table, own_requests, axis=0).reshape(-1)
+    physical = page_table.at[own_requests].get(mode="promise_in_bounds").reshape(-1)
     inverse = jnp.argmax(
         (physical[None, :] == jnp.arange(req_dev * pages_per)[:, None]).astype(jnp.int32), axis=1
     )
-    decode_pages = jnp.take(page_rows, inverse, axis=0)
+    page_start = lax.rem(inverse, pages_per) * PAGE
+    page_length = own_lengths.at[inverse // pages_per].get(mode="promise_in_bounds")
+    alive = page_start[:, None] + jnp.arange(PAGE)[None, :] < page_length[:, None]
+    decode_pages = jnp.where(
+        alive[:, None, :, None],
+        page_rows.at[inverse].get(mode="promise_in_bounds"),
+        jnp.zeros((), jnp.bfloat16),
+    )
     return (layer_out, decode_pages)
 
 

time: 222 us -> 214 us (0.964)
  other arithmetic: 16.6 us -> 7.03 us
  Pallas kernels: 164 us -> 171 us
  local copies, waits for them, and re-layouts: 17.2 us -> 13 us
    pallas_call x1, Pallas kernels: 106 us -> 112 us  [expert_layer(): pl.pallas_call(expert_kernel, out_shape=jax.ShapeDtypeStruct(hidden.shape...]
    unnamed x38 -> x32, local copies, waits for them, and re-layouts: 5.97 us -> 1.78 us
    select_n x5 -> x1, other arithmetic: 4.15 us -> 0.01 us  [on_device(): parcel = handover.at[picked].get(mode='promise_in_bounds')]
    gather x3 -> x4, local copies, waits for them, and re-layouts: 5.4 us -> 5.95 us  [the longest x1 3.09 us: on_device(): parcel = handover.at[picked].get(mode='promise_in_bounds')]
  transfers between devices with their start and end apart: 2 -> 2, of which waited for: 0 -> 0; matrix products, arithmetic and copies ran while one was open for 8% -> 4% of each run, Pallas kernels for 48% -> 53%
where the time goes in v3:
time: 214 us; the launch traced here: 212 us
  Pallas kernels  171 us (80%)
  starting transfers between devices  13.2 us (6%)
  local copies, waits for them, and re-layouts  13 us (6%)
  matrix products  7.06 us (3%)
  other arithmetic  7.03 us (3%)
    pallas_call x1, Pallas kernels, expert_layer(): pl.pallas_call(expert_kernel, out_shape=jax.ShapeDtypeStruct(hidden.shape...  112 us
    pallas_call x1, Pallas kernels, gathered_attention(): pl.pallas_call(functools.partial(attend_kernel, scale, prior_rows, span_r...  58.3 us
    all_to_all x1, starting transfers between devices, on_device(): lax.all_to_all(parcel, 'seq', split_axis=0, concat_axis=0, tiled=True)  9.41 us
  transfers between devices with their start and end apart: 2, of which 0 were waited for; matrix products, arithmetic and copies ran while one was open for 4% of the time, Pallas kernels for 53%

profile of v3, /device:TPU:32, one launch (start us, length us, event | category | flops | bytes accessed | tf_op | source)
XLA Modules:
  0.0 212.5 jit_solution(13568083942756161850)
XLA Ops:
  0.7 1.4 fusion.1
  2.1 0.4 copy-done
  2.5 2.1 fusion.15
  4.5 0.1 multiply_reduce_fusion.1
  4.6 0.3 subtract_convert_fusion
  5.0 0.1 copy.82
  5.1 2.2 %fusion.17 = f32[128,384]{0,1:T(8,128)S(1)} fusion(bf16[2048,384]{1,0:T(8,128)(2,1)} %param.22, bf16[128,2048]{1,0:T(8,128)(2,1)S(1)} %copy-done.1, f32[2048]{0:T(1024)S(1)} %copy-done.8, f32[128]{0:T(128)S(1)} %add_rsqrt_fusion.2), kind=kOutput, calls=%fused_computation.34 | convolution fusion | flops 202375168 | bytes 2302464 | tf_op jit(solution)/shard_map/dot_general | solution.py:820
  7.4 0.6 maximum_bitcast_fusion
  8.0 0.9 copy.83
  8.9 1.2 convolution_convert_fusion.1
  10.2 0.1 multiply_convert_fusion.1
  10.3 0.1 fusion.11.own_ref
  10.4 58.3 %gather_attend.1 = bf16[256,512]{1,0:T(8,128)(2,1)S(1)} custom-call(bf16[256,640]{1,0:T(8,128)(2,1)S(1)} %fusion.10.q_ref, bf16[160,640]{1,0:T(8,128)(2,1)S(1)} %fusion.11.own_ref), custom_call_target="tpu_custom_call" | custom-call | tf_op jit(solution)/shard_map/gather_attend/pallas_call | solution.py:392
  68.6 0.3 convolution_convert_fusion.2
  69.0 1.1 convolution_convert_fusion
  70.1 3.7 %all-to-all-start = ((bf16[4,32,2048]{2,1,0:T(8,128)(2,1)}), bf16[4,32,2048]{2,1,0:T(8,128)(2,1)S(1)}, u32[]{:S(2)}, u32[]{:S(2)}) async-start(bf16[4,32,2048]{2,1,0:T(8,128)(2,1)} %bitcast.7), calls=%async_computation | async-start | bytes 1048576 | tf_op jit(solution)/shard_map/all_to_all | solution.py:29
  73.9 0.1 dynamic_slice.14
  73.9 0.2 convert_reduce_fusion.2
  74.1 0.1 dynamic-slice_add_fusion
  74.2 0.7 iota_reduce_fusion
  74.9 0.1 constant_dynamic-slice_fusion
  75.0 0.7 dynamic_slice.15
  76.4 0.2 dynamic-slice_reduce_fusion
  76.6 0.6 dynamic-slice.6
  77.2 0.1 copy.99
  77.3 0.1 eq.18
  77.4 3.1 %gather_fusion = bf16[64,16,576]{2,1,0:T(8,128)(2,1)} fusion(bf16[64,16,576]{2,1,0:T(8,128)(2,1)} %bitcast.37, s32[1024]{0:T(1024)S(1)} %pad_clamp_fusion.1), kind=kCustom, calls=%fused_computation | custom fusion | bytes 2359552 | tf_op jit(solution)/shard_map/gather | solution.py:896
  80.5 0.6 iota_reduce_fusion.1
  81.1 0.7 add_compare_fusion
  81.8 9.4 %all-to-all-start.1 = ((bf16[64,1,16,576]{3,2,1,0:T(8,128)(2,1)}), bf16[64,1,16,576]{3,2,1,0:T(8,128)(2,1)}, u32[]{:S(2)}, u32[]{:S(2)}) async-start(bf16[64,1,16,576]{3,2,1,0:T(8,128)(2,1)} %bitcast.34), calls=%async_computation.1 | async-start | bytes 2621440 | tf_op jit(solution)/shard_map/all_to_all | solution.py:897
  91.2 0.2 convert_reduce_fusion.1
  91.4 0.1 reduce_sum.79
  91.6 0.1 convert_reduce_fusion
  91.7 0.2 multiply_reduce_fusion
  91.8 0.1 copy-done.9
  91.9 0.1 multiply_convert_fusion
  92.0 0.5 copy-done.6
  92.5 0.2 fusion.24
  92.7 0.2 select_reduce_fusion
  92.9 0.1 copy.90
  93.0 0.1 fusion.21
  93.1 0.1 fusion.20
  93.2 0.7 concatenate.29.rows_ref
  94.0 112.3 %experts.1 = bf16[32,2048]{1,0:T(8,128)(2,1)} custom-call(bf16[32,2176]{1,0:T(8,128)(2,1)} %concatenate.29.rows_ref, f32[32,2048]{1,0:T(8,128)} %copy-done.2, bf16[1,352,2048]{2,1,0:T(8,128)(2,1)} %bitcast.35, bf16[1,352,2048]{2,1,0:T(8,128)(2,1)} %bitcast.36, bf16[1,352,2048]{2,1,0:T(8,128)(2,1)} %wd_hbm.1), custom_call_target="tpu_custom_call" | custom-call | tf_op jit(solution)/shard_map/experts/pallas_call | solution.py:735
  206.3 2.4 %copy.93 = bf16[8,128,576]{1,2,0:T(8,128)(2,1)} copy(bf16[8,128,576]{2,1,0:T(8,128)(2,1)} %bitcast.15) | data formatting | bytes 2359296 | tf_op jit(solution)/shard_map/reshape;transpose;reshape;reshape;transpose;reshape | solution.py:915
  208.7 2.0 gather_fusion.1
  210.7 1.1 fusion
  211.8 0.7 copy.101
  (44 shorter events, 0.3 us)
Async XLA Ops:
  0.6 1.8 copy-start
  2.5 2.6 %copy-start.1 = (bf16[128,2048]{1,0:T(8,128)(2,1)S(1)}, bf16[128,2048]{1,0:T(8,128)(2,1)}, u32[]{:S(2)}) copy-start(bf16[128,2048]{1,0:T(8,128)(2,1)} %param.19) | copy-start | bytes 1572868
  2.5 2.6 %copy-start.8 = (f32[2048]{0:T(1024)S(1)}, f32[2048]{0:T(1024)}, u32[]{:S(2)}) copy-start(f32[2048]{0:T(1024)} %param.21) | copy-start | bytes 24580
  7.3 2.8 %copy-start.11 = (f32[512]{0:T(512)S(1)}, f32[512]{0:T(512)}, u32[]{:S(2)}) copy-start(f32[512]{0:T(512)} %param.24) | copy-start | bytes 6148
  8.8 1.4 copy-start.7
  10.1 58.5 %copy-start.5 = (bf16[2,512,128]{2,1,0:T(8,128)(2,1)S(1)}, bf16[2,512,128]{2,1,0:T(8,128)(2,1)}, u32[]{:S(2)}) copy-start(bf16[2,512,128]{2,1,0:T(8,128)(2,1)} %param.26) | copy-start | bytes 786436
  10.1 58.8 %copy-start.3 = (bf16[256,2048]{1,0:T(8,128)(2,1)S(1)}, bf16[256,2048]{1,0:T(8,128)(2,1)}, u32[]{:S(2)}) copy-start(bf16[256,2048]{1,0:T(8,128)(2,1)} %param.27) | copy-start | bytes 3145732
  68.9 4.9 %copy-start.13 = (s32[256]{0:T(256)S(1)}, s32[256]{0:T(256)}, u32[]{:S(2)}) copy-start(s32[256]{0:T(256)} %param.36) | copy-start | bytes 3076
  68.9 6.0 %copy-start.10 = (s32[128,6]{0,1:T(8,128)S(1)}, s32[128,6]{0,1:T(8,128)}, u32[]{:S(2)}) copy-start(s32[128,6]{0,1:T(8,128)} %param.30) | copy-start | bytes 9220
  69.0 7.4 %copy-start.12 = (s32[256,8]{0,1:T(8,128)S(1)}, s32[256,8]{0,1:T(8,128)}, u32[]{:S(2)}) copy-start(s32[256,8]{0,1:T(8,128)} %param.37) | copy-start | bytes 24580
  69.0 7.6 %copy-start.14 = (s32[256]{0:T(256)S(1)}, s32[256]{0:T(256)}, u32[]{:S(2)}) copy-start(s32[256]{0:T(256)} %param.35) | copy-start | bytes 3076
  70.1 11.7 %all-to-all-start = ((bf16[4,32,2048]{2,1,0:T(8,128)(2,1)}), bf16[4,32,2048]{2,1,0:T(8,128)(2,1)S(1)}, u32[]{:S(2)}, u32[]{:S(2)}) async-start(bf16[4,32,2048]{2,1,0:T(8,128)(2,1)} %bitcast.7), calls=%async_computation | async-start | bytes 1048576 | tf_op jit(solution)/shard_map/all_to_all | solution.py:29
  81.8 124.4 %all-to-all-start.1 = ((bf16[64,1,16,576]{3,2,1,0:T(8,128)(2,1)}), bf16[64,1,16,576]{3,2,1,0:T(8,128)(2,1)}, u32[]{:S(2)}, u32[]{:S(2)}) async-start(bf16[64,1,16,576]{3,2,1,0:T(8,128)(2,1)} %bitcast.34), calls=%async_computation.1 | async-start | bytes 2621440 | tf_op jit(solution)/shard_map/all_to_all | solution.py:897
  91.2 0.7 copy-start.9
  91.5 1.0 copy-start.6
  91.8 2.1 %copy-start.2 = (f32[32,2048]{1,0:T(8,128)}, f32[32,2048]{1,0:T(8,128)S(1)}, u32[]{:S(2)}) copy-start(f32[32,2048]{1,0:T(8,128)S(1)} %get-tuple-element.41.hidden_ref) | copy-start | bytes 786436
  210.7 1.1 copy-start.4
